TPU v7x, 32 devices: a whole 2x2x4 slice. The times are simulated.
32 devices in a mesh: ens: 2 (over y), gy: 4 (over z), gx: 4 (over x, core).
Axes of the slice: x: 2, y: 2, z: 4, core: 2. Of those that a mesh axis runs over, the one named last changes fastest.
Arguments:
- base_stream: float32 [4, 32, 512], P('ens', 'gy', 'gx'), parts along dimension 0, may hold values from -6 to 6
- tangent_vectors: float32 [64, 2, 32, 512], P('ens', None, 'gy', 'gx'), parts along dimension 0, may hold values from -40 to 40, as said below
Outputs:
- basis_vectors: float32 [64, 2, 32, 512], P('ens', None, 'gy', 'gx'), parts along dimension 0
- upper_factor: float32 [64, 32], P('ens'), parts along dimension 0
There are 2 independent parts, one for each index of `ens`. A program takes and returns all parts, laid end to end along the dimension named above; each array names one. Nothing has to cross between parts.
Inputs may be any that keep to these rules, and one draw needn't show every extreme that they name: `tangent_vectors`: Real-valued; the vectors are linearly independent.
All inputs are finite; a program needn't handle non-finite values.
Results may differ from a plain program's by a relative error of at most 0.0003.
Values sent between devices are 32-bit elements; how exact they have to be, the bound alone decides.
No kernel may reach another device: no remote copies, remote signals or barrier semaphores. Data moves between devices by JAX's collectives and lax.ppermute only.
A program may use at most 64 MiB of HBM per device.

v0:
```python
import jax
import jax.numpy as jnp
from jax import lax
from jax.sharding import PartitionSpec as P

coupling_top = 0.6
coupling_bottom = 0.3
time_step = 0.05
hyper_visc = 0.1


def padded(cells, sides, width):
    for axis, dim in sides:
        count = lax.axis_size(axis)
        head = lax.slice_in_dim(cells, 0, width, axis=dim)
        tail = lax.slice_in_dim(cells, cells.shape[dim] - width, cells.shape[dim], axis=dim)
        cells = jnp.concatenate(
            [
                lax.ppermute(tail, axis, [(i, (i + 1) % count) for i in range(count)]),
                cells,
                lax.ppermute(head, axis, [((i + 1) % count, i) for i in range(count)]),
            ],
            axis=dim,
        )
    return cells


def combined_all(value, axis, join):
    pieces = lax.all_gather(value, axis)
    head = pieces[0]
    tail = pieces[1:]
    running, _ = lax.scan(lambda running, slab: (join(running, slab), None), head, tail)
    return running


def inner_part(values):
    return values[..., 1:-1, 1:-1]


def padded_neighbours(values):
    return (
        values[..., 1:-1, :-2]
        + values[..., 1:-1, 2:]
        + values[..., :-2, 1:-1]
        + values[..., 2:, 1:-1]
    )


def padded_laplacian(values):
    return padded_neighbours(values) - 4.0 * inner_part(values)


def padded_cols(values):
    return values[..., 1:-1, 2:] - values[..., 1:-1, :-2]


def padded_rows(values):
    return values[..., 2:, 1:-1] - values[..., :-2, 1:-1]


def padded_jacobian(first, second):
    return (
        padded_cols(first) * padded_rows(second) - padded_rows(first) * padded_cols(second)
    ) * 0.25


def coupling_array():
    return jnp.array([coupling_top, coupling_bottom], jnp.float32).reshape(2, 1, 1)


def padded_relax(stream_ext, potential):
    coupling = coupling_array()
    return (
        padded_neighbours(stream_ext) + coupling * jnp.flip(inner_part(stream_ext), -3) - potential
    ) / (4.0 + coupling)


def pv_halo(potential):
    return padded(potential, (("gy", 2), ("gx", 3)), 2)


def combine_factors(left_factor, right_factor):
    summed = jnp.dot(
        left_factor.T,
        left_factor,
        precision=lax.Precision.HIGHEST,
        preferred_element_type=jnp.float32,
    )
    summed = summed + jnp.dot(
        right_factor.T,
        right_factor,
        precision=lax.Precision.HIGHEST,
        preferred_element_type=jnp.float32,
    )
    return jnp.linalg.cholesky(summed).T


def base_fields(base_ext):
    coupling = coupling_array()
    base_cycle = inner_part(base_ext)
    base_pv = padded_laplacian(base_ext) - coupling * (base_cycle - jnp.flip(base_cycle, -3))
    return (base_cycle, base_pv)


def tendency_of(pv_wide, stream_cycle, base_cycle, base_pv):
    pv_cycle = inner_part(pv_wide)
    return (
        -padded_jacobian(base_cycle, pv_cycle)
        - padded_jacobian(stream_cycle, base_pv)
        - hyper_visc * padded_laplacian(padded_laplacian(pv_wide))
    )


def local(base_stream, tangent_vectors):
    coupling = coupling_array()
    base_ext = padded(base_stream, (("gy", 1), ("gx", 2)), 2)
    base_cycle, base_pv = base_fields(base_ext)
    potential = tangent_vectors
    pv_wide = pv_halo(potential)
    stream_wide = -pv_wide / (4.0 + coupling)
    stream_cycle = padded_relax(stream_wide, inner_part(pv_wide))
    potential = potential + time_step * tendency_of(pv_wide, stream_cycle, base_cycle, base_pv)
    cells = potential.shape[1] * potential.shape[2] * potential.shape[3]
    total = 1.0 * cells * lax.axis_size("gy") * lax.axis_size("gx")
    columns = potential.reshape(potential.shape[0], cells)
    local_gram = (
        jnp.dot(
            columns, columns.T, precision=lax.Precision.HIGHEST, preferred_element_type=jnp.float32
        )
        / total
    )
    local_upper = jnp.linalg.cholesky(local_gram).T
    upper = combined_all(local_upper, ("gy", "gx"), combine_factors)
    lower = upper.T
    basis = lax.linalg.triangular_solve(lower, columns, left_side=True, lower=True)
    return (basis.reshape(potential.shape), upper)


def solution(mesh):
    return jax.shard_map(
        local,
        mesh=mesh,
        in_specs=(P("ens", "gy", "gx"), P("ens", None, "gy", "gx")),
        out_specs=(P("ens", None, "gy", "gx"), P("ens", None)),
        check_vma=False,
    )
```

profile of v0, /device:TPU:0, one launch (start us, length us, event | category | flops | bytes accessed | tf_op | source)
XLA Modules:
  0.0 134.5 jit_solution(5237825671170848654)
XLA Ops:
  0.6 0.8 fusion.40
  1.4 3.1 %collective-permute-start = (f32[2,2,128]{2,1,0:T(2,128)S(1)}, f32[2,2,128]{2,1,0:T(2,128)S(1)}, u32[]{:S(2)}, u32[]{:S(2)}) collective-permute-start(f32[2,2,128]{2,1,0:T(2,128)S(1)} %get-tuple-element.56), channel_id=1, source_target_pairs={{0,4},{4,8},{8,12},{12,0},{1,5},{5,9},{9,13},{13,1},{2,6},{6,10},{... | collective-permute-start | bytes 6152 | tf_op jit(solution)/shard_map/ppermute | solution.py:19
  4.5 2.0 %collective-permute-start.1 = (f32[2,2,128]{2,1,0:T(2,128)S(1)}, f32[2,2,128]{2,1,0:T(2,128)S(1)}, u32[]{:S(2)}, u32[]{:S(2)}) collective-permute-start(f32[2,2,128]{2,1,0:T(2,128)S(1)} %get-tuple-element.57), channel_id=1, source_target_pairs={{4,0},{8,4},{12,8},{0,12},{5,1},{9,5},{13,9},{1,13},{6,2},{10,6},{... | collective-permute-start | bytes 6152 | tf_op jit(solution)/shard_map/ppermute | solution.py:21
  6.5 1.1 fusion.38
  7.6 2.1 %collective-permute-start.4 = (f32[32,2,2,128]{3,2,1,0:T(2,128)S(1)}, f32[32,2,2,128]{3,2,1,0:T(2,128)S(1)}, u32[]{:S(2)}, u32[]{:S(2)}) collective-permute-start(f32[32,2,2,128]{3,2,1,0:T(2,128)S(1)} %get-tuple-element.49), channel_id=1, source_target_pairs={{4,0},{8,4},{12,8},{0,12},{5,1},{9,5},{13,9},{1,13},{6,2},{10,6},{... | collective-permute-start | bytes 196616 | tf_op jit(solution)/shard_map/ppermute | solution.py:21
  10.3 1.0 collective-permute-done.2
  11.3 1.7 %collective-permute-done.3 = f32[2,12,2]{2,1,0:T(8,128)S(1)} collective-permute-done((f32[2,12,2]{2,1,0:T(8,128)S(1)}, f32[2,12,2]{2,1,0:T(8,128)S(1)}, u32[]{:S(2)}, u32[]{:S(2)}) %collective-permute-start.3) | collective-permute-done | bytes 224 | tf_op jit(solution)/shard_map/ppermute | solution.py:19
  13.4 2.4 %collective-permute-done.5 = f32[32,2,2,128]{3,2,1,0:T(2,128)S(1)} collective-permute-done((f32[32,2,2,128]{3,2,1,0:T(2,128)S(1)}, f32[32,2,2,128]{3,2,1,0:T(2,128)S(1)}, u32[]{:S(2)}, u32[]{:S(2)}) %collective-permute-start.5) | collective-permute-done | bytes 65568 | tf_op jit(solution)/shard_map/ppermute | solution.py:19
  16.7 10.7 %collective-permute-done.6 = f32[32,2,12,2]{3,2,1,0:T(8,128)S(1)} collective-permute-done((f32[32,2,12,2]{3,2,1,0:T(8,128)S(1)}, f32[32,2,12,2]{3,2,1,0:T(8,128)S(1)}, u32[]{:S(2)}, u32[]{:S(2)}) %collective-permute-start.6) | collective-permute-done | bytes 6176 | tf_op jit(solution)/shard_map/ppermute | solution.py:21
  27.4 2.9 %collective-permute-done.7 = f32[32,2,12,2]{3,2,1,0:T(8,128)S(1)} collective-permute-done((f32[32,2,12,2]{3,2,1,0:T(8,128)S(1)}, f32[32,2,12,2]{3,2,1,0:T(8,128)S(1)}, u32[]{:S(2)}, u32[]{:S(2)}) %collective-permute-start.7) | collective-permute-done | bytes 6176 | tf_op jit(solution)/shard_map/ppermute | solution.py:19
  30.4 0.8 negate_multiply_fusion
  31.5 2.3 %fusion.9 = (f32[32,2,10,130]{3,2,1,0:T(8,128)S(1)}, f32[32,2,10,130]{3,2,1,0:T(8,128)S(1)}) fusion(f32[32,2,12,132]{3,2,1,0:T(8,128)S(1)} %get-tuple-element.42, f32[32,2,10,130]{3,2,1,0:T(8,128)S(1)} %slice.229, f32[32,2,12,132]{3,2,1,0:T(8,128)S(1)} %get-tuple-element.43, f32[2]{0:T(128)S(1)} %copy-done.3, f32[2]{0:T(128)S(1)} %copy-done.2, ...), kind=kLoop, calls=%fused_computation.26 | loop fusion | flops 1497600 | bytes 3733520 | tf_op jit(solution)/shard_map/div | solution.py:73
  33.8 1.0 fusion.14
  35.3 2.9 %cholesky.55 = f32[32,32]{1,0:T(8,128)S(1)} custom-call(f32[32,32]{1,0:T(8,128)S(1)} %fusion.35), custom_call_target="Cholesky" | custom-call | tf_op jit(solution)/shard_map/jit(cholesky)/cholesky | solution.py:132
  38.2 0.6 compare_reduce_fusion.1
  38.9 0.6 select_bitcast_fusion.1
  39.6 19.4 %all-gather = f32[512,32]{1,0:T(8,128)S(1)} all-gather(f32[32,32]{1,0:T(8,128)S(1)} %copy.37), channel_id=2, replica_groups=mesh['ens'=2,'gy'=4,'gx'=4] {'gy','gx'}, dimensions={0}, use_global_device_ids=true | all-gather | bytes 69632 | tf_op jit(solution)/shard_map/all_gather | solution.py:29
  59.1 70.9 %while.10 = (s32[]{:T(128)}, f32[32,32]{0,1:T(8,128)S(1)}, f32[15,32,32]{2,1,0:T(8,128)S(1)}, s32[]{:T(128)}) while((s32[]{:T(128)}, f32[32,32]{0,1:T(8,128)S(1)}, f32[15,32,32]{2,1,0:T(8,128)S(1)}, s32[]{:T(128)}) %tuple.42), condition=%wide.region_3.5_spmd, body=%wide.region_2.4_spmd.sunk | while | flops 795681 | bytes 78139 | solution.py:32
  59.6 2.9 %cholesky.118 = f32[32,32]{1,0:T(8,128)S(1)} custom-call(f32[32,32]{1,0:T(8,128)S(1)} %fusion.53), custom_call_target="Cholesky" | custom-call | tf_op jit(solution)/shard_map/while/body/eval_jaxpr/jit(cholesky)/cholesky | solution.py:95
  62.5 0.6 compare_reduce_fusion.3
  63.2 0.6 select_bitcast_fusion.3
  64.3 2.9 %cholesky.118 = f32[32,32]{1,0:T(8,128)S(1)} custom-call(f32[32,32]{1,0:T(8,128)S(1)} %fusion.53), custom_call_target="Cholesky" | custom-call | tf_op jit(solution)/shard_map/while/body/eval_jaxpr/jit(cholesky)/cholesky | solution.py:95
  67.2 0.6 compare_reduce_fusion.3
  67.9 0.6 select_bitcast_fusion.3
  69.0 2.9 %cholesky.118 = f32[32,32]{1,0:T(8,128)S(1)} custom-call(f32[32,32]{1,0:T(8,128)S(1)} %fusion.53), custom_call_target="Cholesky" | custom-call | tf_op jit(solution)/shard_map/while/body/eval_jaxpr/jit(cholesky)/cholesky | solution.py:95
  72.0 0.6 compare_reduce_fusion.3
  72.6 0.6 select_bitcast_fusion.3
  73.7 2.9 %cholesky.118 = f32[32,32]{1,0:T(8,128)S(1)} custom-call(f32[32,32]{1,0:T(8,128)S(1)} %fusion.53), custom_call_target="Cholesky" | custom-call | tf_op jit(solution)/shard_map/while/body/eval_jaxpr/jit(cholesky)/cholesky | solution.py:95
  76.7 0.6 compare_reduce_fusion.3
  77.3 0.6 select_bitcast_fusion.3
  78.5 2.9 %cholesky.118 = f32[32,32]{1,0:T(8,128)S(1)} custom-call(f32[32,32]{1,0:T(8,128)S(1)} %fusion.53), custom_call_target="Cholesky" | custom-call | tf_op jit(solution)/shard_map/while/body/eval_jaxpr/jit(cholesky)/cholesky | solution.py:95
  81.4 0.6 compare_reduce_fusion.3
  82.1 0.6 select_bitcast_fusion.3
  83.2 2.9 %cholesky.118 = f32[32,32]{1,0:T(8,128)S(1)} custom-call(f32[32,32]{1,0:T(8,128)S(1)} %fusion.53), custom_call_target="Cholesky" | custom-call | tf_op jit(solution)/shard_map/while/body/eval_jaxpr/jit(cholesky)/cholesky | solution.py:95
  86.1 0.6 compare_reduce_fusion.3
  86.8 0.6 select_bitcast_fusion.3
  87.9 2.9 %cholesky.118 = f32[32,32]{1,0:T(8,128)S(1)} custom-call(f32[32,32]{1,0:T(8,128)S(1)} %fusion.53), custom_call_target="Cholesky" | custom-call | tf_op jit(solution)/shard_map/while/body/eval_jaxpr/jit(cholesky)/cholesky | solution.py:95
  90.9 0.6 compare_reduce_fusion.3
  91.5 0.6 select_bitcast_fusion.3
  92.6 2.9 %cholesky.118 = f32[32,32]{1,0:T(8,128)S(1)} custom-call(f32[32,32]{1,0:T(8,128)S(1)} %fusion.53), custom_call_target="Cholesky" | custom-call | tf_op jit(solution)/shard_map/while/body/eval_jaxpr/jit(cholesky)/cholesky | solution.py:95
  95.6 0.6 compare_reduce_fusion.3
  96.2 0.6 select_bitcast_fusion.3
  97.4 2.9 %cholesky.118 = f32[32,32]{1,0:T(8,128)S(1)} custom-call(f32[32,32]{1,0:T(8,128)S(1)} %fusion.53), custom_call_target="Cholesky" | custom-call | tf_op jit(solution)/shard_map/while/body/eval_jaxpr/jit(cholesky)/cholesky | solution.py:95
  100.3 0.6 compare_reduce_fusion.3
  101.0 0.6 select_bitcast_fusion.3
  102.1 2.9 %cholesky.118 = f32[32,32]{1,0:T(8,128)S(1)} custom-call(f32[32,32]{1,0:T(8,128)S(1)} %fusion.53), custom_call_target="Cholesky" | custom-call | tf_op jit(solution)/shard_map/while/body/eval_jaxpr/jit(cholesky)/cholesky | solution.py:95
  105.0 0.6 compare_reduce_fusion.3
  105.7 0.6 select_bitcast_fusion.3
  106.8 2.9 %cholesky.118 = f32[32,32]{1,0:T(8,128)S(1)} custom-call(f32[32,32]{1,0:T(8,128)S(1)} %fusion.53), custom_call_target="Cholesky" | custom-call | tf_op jit(solution)/shard_map/while/body/eval_jaxpr/jit(cholesky)/cholesky | solution.py:95
  109.8 0.6 compare_reduce_fusion.3
  110.4 0.6 select_bitcast_fusion.3
  111.5 2.9 %cholesky.118 = f32[32,32]{1,0:T(8,128)S(1)} custom-call(f32[32,32]{1,0:T(8,128)S(1)} %fusion.53), custom_call_target="Cholesky" | custom-call | tf_op jit(solution)/shard_map/while/body/eval_jaxpr/jit(cholesky)/cholesky | solution.py:95
  114.5 0.6 compare_reduce_fusion.3
  115.1 0.6 select_bitcast_fusion.3
  116.3 2.9 %cholesky.118 = f32[32,32]{1,0:T(8,128)S(1)} custom-call(f32[32,32]{1,0:T(8,128)S(1)} %fusion.53), custom_call_target="Cholesky" | custom-call | tf_op jit(solution)/shard_map/while/body/eval_jaxpr/jit(cholesky)/cholesky | solution.py:95
  119.9 0.6 select_bitcast_fusion.3
  121.0 2.9 %cholesky.118 = f32[32,32]{1,0:T(8,128)S(1)} custom-call(f32[32,32]{1,0:T(8,128)S(1)} %fusion.53), custom_call_target="Cholesky" | custom-call | tf_op jit(solution)/shard_map/while/body/eval_jaxpr/jit(cholesky)/cholesky | solution.py:95
  124.6 0.6 select_bitcast_fusion.3
  125.7 2.9 %cholesky.118 = f32[32,32]{1,0:T(8,128)S(1)} custom-call(f32[32,32]{1,0:T(8,128)S(1)} %fusion.53), custom_call_target="Cholesky" | custom-call | tf_op jit(solution)/shard_map/while/body/eval_jaxpr/jit(cholesky)/cholesky | solution.py:95
  128.7 0.6 compare_reduce_fusion.3
  129.3 0.6 select_bitcast_fusion.3
  130.0 0.7 copy.44
  130.7 2.4 %custom-call.5 = f32[1,32,32]{1,2,0:T(8,128)S(1)} custom-call(f32[1,32,32]{2,1,0:T(8,128)S(1)} %fusion.34), custom_call_target="InvertDiagBlocksLowerTriangular" | custom-call | tf_op jit(solution)/shard_map/triangular_solve | solution.py:135
  133.7 0.9 copy.43
  (114 shorter events, 11.8 us)
Async XLA Ops:
  1.4 8.3 %collective-permute-start = (f32[2,2,128]{2,1,0:T(2,128)S(1)}, f32[2,2,128]{2,1,0:T(2,128)S(1)}, u32[]{:S(2)}, u32[]{:S(2)}) collective-permute-start(f32[2,2,128]{2,1,0:T(2,128)S(1)} %get-tuple-element.56), channel_id=1, source_target_pairs={{0,4},{4,8},{8,12},{12,0},{1,5},{5,9},{9,13},{13,1},{2,6},{6,10},{... | collective-permute-start | bytes 6152 | tf_op jit(solution)/shard_map/ppermute | solution.py:19
  4.5 5.2 %collective-permute-start.1 = (f32[2,2,128]{2,1,0:T(2,128)S(1)}, f32[2,2,128]{2,1,0:T(2,128)S(1)}, u32[]{:S(2)}, u32[]{:S(2)}) collective-permute-start(f32[2,2,128]{2,1,0:T(2,128)S(1)} %get-tuple-element.57), channel_id=1, source_target_pairs={{4,0},{8,4},{12,8},{0,12},{5,1},{9,5},{13,9},{1,13},{6,2},{10,6},{... | collective-permute-start | bytes 6152 | tf_op jit(solution)/shard_map/ppermute | solution.py:21
  6.5 3.2 %copy-start.1 = (f32[2,8,128]{2,1,0:T(8,128)S(1)}, f32[2,8,128]{2,1,0:T(8,128)}, u32[]{:S(2)}) copy-start(f32[2,8,128]{2,1,0:T(8,128)} %param.8) | copy-start | bytes 24580
  6.5 6.7 %copy-start.2 = (f32[2]{0:T(128)S(1)}, f32[2]{0:T(128)}, u32[]{:S(2)}) copy-start(f32[2]{0:T(128)} %constant.56.clone) | copy-start | bytes 28
  7.6 8.2 %copy-start = (f32[32,2,8,128]{3,2,1,0:T(8,128)S(1)}, f32[32,2,8,128]{3,2,1,0:T(8,128)}, u32[]{:S(2)}) copy-start(f32[32,2,8,128]{3,2,1,0:T(8,128)} %param.9) | copy-start | bytes 786436
  7.6 5.8 %collective-permute-start.4 = (f32[32,2,2,128]{3,2,1,0:T(2,128)S(1)}, f32[32,2,2,128]{3,2,1,0:T(2,128)S(1)}, u32[]{:S(2)}, u32[]{:S(2)}) collective-permute-start(f32[32,2,2,128]{3,2,1,0:T(2,128)S(1)} %get-tuple-element.49), channel_id=1, source_target_pairs={{4,0},{8,4},{12,8},{0,12},{5,1},{9,5},{13,9},{1,13},{6,2},{10,6},{... | collective-permute-start | bytes 196616 | tf_op jit(solution)/shard_map/ppermute | solution.py:21
  9.7 6.1 %collective-permute-start.5 = (f32[32,2,2,128]{3,2,1,0:T(2,128)S(1)}, f32[32,2,2,128]{3,2,1,0:T(2,128)S(1)}, u32[]{:S(2)}, u32[]{:S(2)}) collective-permute-start(f32[32,2,2,128]{3,2,1,0:T(2,128)S(1)} %get-tuple-element.48), channel_id=1, source_target_pairs={{0,4},{4,8},{8,12},{12,0},{1,5},{5,9},{9,13},{13,1},{2,6},{6,10},{... | collective-permute-start | bytes 196616 | tf_op jit(solution)/shard_map/ppermute | solution.py:19
  9.8 1.5 %collective-permute-start.2 = (f32[2,12,2]{2,1,0:T(8,128)S(1)}, f32[2,12,2]{2,1,0:T(8,128)S(1)}, u32[]{:S(2)}, u32[]{:S(2)}) collective-permute-start(f32[2,12,2]{2,1,0:T(8,128)S(1)} %get-tuple-element.53), channel_id=1, source_target_pairs={{1,0},{2,1},{3,2},{0,3},{5,4},{6,5},{7,6},{4,7},{9,8},{10,9},{11,1... | collective-permute-start | bytes 584 | tf_op jit(solution)/shard_map/ppermute | solution.py:21
  9.9 3.2 %collective-permute-start.3 = (f32[2,12,2]{2,1,0:T(8,128)S(1)}, f32[2,12,2]{2,1,0:T(8,128)S(1)}, u32[]{:S(2)}, u32[]{:S(2)}) collective-permute-start(f32[2,12,2]{2,1,0:T(8,128)S(1)} %get-tuple-element.52), channel_id=1, source_target_pairs={{0,1},{1,2},{2,3},{3,0},{4,5},{5,6},{6,7},{7,4},{8,9},{9,10},{10,1... | collective-permute-start | bytes 584 | tf_op jit(solution)/shard_map/ppermute | solution.py:19
  16.1 11.4 %collective-permute-start.6 = (f32[32,2,12,2]{3,2,1,0:T(8,128)S(1)}, f32[32,2,12,2]{3,2,1,0:T(8,128)S(1)}, u32[]{:S(2)}, u32[]{:S(2)}) collective-permute-start(f32[32,2,12,2]{3,2,1,0:T(8,128)S(1)} %get-tuple-element.47), channel_id=1, source_target_pairs={{1,0},{2,1},{3,2},{0,3},{5,4},{6,5},{7,6},{4,7},{9,8},{10,9},{11,1... | collective-permute-start | bytes 18440 | tf_op jit(solution)/shard_map/ppermute | solution.py:21
  16.1 14.3 %copy-start.3 = (f32[2]{0:T(128)S(1)}, f32[2]{0:T(128)}, u32[]{:S(2)}) copy-start(f32[2]{0:T(128)} %constant.58) | copy-start | bytes 28
  16.1 14.2 %collective-permute-start.7 = (f32[32,2,12,2]{3,2,1,0:T(8,128)S(1)}, f32[32,2,12,2]{3,2,1,0:T(8,128)S(1)}, u32[]{:S(2)}, u32[]{:S(2)}) collective-permute-start(f32[32,2,12,2]{3,2,1,0:T(8,128)S(1)} %get-tuple-element.46), channel_id=1, source_target_pairs={{0,1},{1,2},{2,3},{3,0},{4,5},{5,6},{6,7},{7,4},{8,9},{9,10},{10,1... | collective-permute-start | bytes 18440 | tf_op jit(solution)/shard_map/ppermute | solution.py:19
where the time goes:
time: 135 us
  other arithmetic  74.9 us (55%)
  blocking collectives  19.4 us (14%)
  waiting for transfers between devices  18.8 us (14%)
  starting transfers between devices  8.21 us (6%)
  matrix products  6.21 us (5%)
  local copies, waits for them, and re-layouts  5.6 us (4%)
    another operation x45, other arithmetic, combine_factors(): return jnp.linalg.cholesky(summed).T  53.9 us
    all_gather x1, blocking collectives, combined_all(): pieces = lax.all_gather(value, axis)  19.4 us
    ppermute x4, waiting for transfers between devices, padded(): lax.ppermute(head, axis, [((i + 1) % count, i) for i in range(count)])  11.8 us
    transpose x15, other arithmetic, combine_factors(): return jnp.linalg.cholesky(summed).T  9.74 us
    ppermute x4, waiting for transfers between devices, padded(): lax.ppermute(tail, axis, [(i, (i + 1) % count) for i in range(count)])  7.05 us
    ppermute x4, starting transfers between devices, padded(): lax.ppermute(head, axis, [((i + 1) % count, i) for i in range(count)])  4.25 us
    ppermute x4, starting transfers between devices, padded(): lax.ppermute(tail, axis, [(i, (i + 1) % count) for i in range(count)])  3.96 us
    another operation x3, other arithmetic, local(): local_upper = jnp.linalg.cholesky(local_gram).T  3.6 us
  transfers between devices with their start and end apart: 8, of which 5 were waited for; matrix products, arithmetic and copies ran while one was open for 1% of the time, Pallas kernels for 0%

commit v1 on v0

v1 whole, which is shorter than its diff:
```python
import jax
import jax.numpy as jnp
from jax import lax
from jax.experimental import pallas as pl
from jax.experimental.pallas import tpu as pltpu
from jax.sharding import PartitionSpec as P

coupling_pair = (0.6, 0.3)
time_step = 0.05
hyper_visc = 0.1

SUB = 8
VMEM = pl.BlockSpec(memory_space=pltpu.VMEM)


def pairings(value_a, value_b, axis):
    count = lax.axis_size(axis)
    got_b = lax.ppermute(value_b, axis, [(i, (i + 1 if i % 2 else i - 1) % count) for i in range(count)])
    got_a = lax.ppermute(value_a, axis, [(i, (i + 1 if i % 2 == 0 else i - 1) % count) for i in range(count)])
    return got_a, got_b


def is_even(axis):
    return lax.rem(lax.axis_index(axis), 2) == 0


def lanes_of(shape):
    return lax.broadcasted_iota(jnp.int32, shape, len(shape) - 1)


class Rows:
    def __init__(self, sizes, pv, base, got_a, got_b):
        self.vectors, self.layers, self.rows, self.columns = sizes
        self.groups = self.vectors // SUB
        self.pv, self.base, self.got_a, self.got_b = pv, base, got_a, got_b
        self.even = is_even("gy")

    def halo(self, side, layer, step, group):
        if group < self.groups:
            at = pl.ds((layer * 2 + step) * self.vectors + group * SUB, SUB)
        else:
            at = pl.ds(self.layers * 2 * self.vectors + layer * 2 + step, 1)
        first, second = self.got_a[at, :], self.got_b[at, :]
        found = jnp.where(self.even, second, first) if side == "above" else jnp.where(self.even, first, second)
        return jnp.broadcast_to(found, (SUB, self.columns))

    def own(self, layer, row, group):
        if group < self.groups:
            stride = self.layers * self.rows
            return self.pv[pl.ds(group * SUB * stride + layer * self.rows + row, SUB, stride=stride), :]
        return jnp.broadcast_to(self.base[pl.ds(layer * self.rows + row, 1), :], (SUB, self.columns))

    def get(self, layer, row, group):
        if row < 0:
            return self.halo("above", layer, row + 2, group)
        if row >= self.rows:
            return self.halo("below", layer, row - self.rows, group)
        return self.own(layer, row, group)


def pack_rows_body(sizes, pv, base, out_a, out_b):
    vectors, layers, rows, columns = sizes
    source = Rows(sizes, pv, base, None, None)
    for layer in range(layers):
        for step in range(2):
            for group in range(source.groups + 1):
                top = source.own(layer, step, group)
                bottom = source.own(layer, rows - 2 + step, group)
                if group < source.groups:
                    at = pl.ds((layer * 2 + step) * vectors + group * SUB, SUB)
                else:
                    at = pl.ds(layers * 2 * vectors + layer * 2 + step, 1)
                    top, bottom = top[:1], bottom[:1]
                out_a[at, :] = jnp.where(source.even, bottom, top)
                out_b[at, :] = jnp.where(source.even, top, bottom)
    left = pl.ds(layers * 2 * (vectors + 1), SUB - layers * 2)
    out_a[left, :] = jnp.zeros((SUB - layers * 2, columns), jnp.float32)
    out_b[left, :] = jnp.zeros((SUB - layers * 2, columns), jnp.float32)


def pack_columns_body(sizes, pv, base, got_a, got_b, out):
    vectors, layers, rows, columns = sizes
    source = Rows(sizes, pv, base, got_a, got_b)
    spot = lanes_of((SUB, columns)) // 4
    for group in range(source.groups + 1):
        total = jnp.zeros((SUB, columns), jnp.float32)
        for layer in range(layers):
            for row in range(-1, rows + 1):
                place = layer * (rows + 2) + row + 1
                turned = pltpu.roll(source.get(layer, row, group), (2 + 4 * place) % columns, 1)
                total = jnp.where(spot == place, turned, total)
        out[pl.ds(group * SUB, SUB), :] = total


def stencil_body(sizes, scale, pv, base, got_a, got_b, side_a, side_b, evolved, gram, coef):
    vectors, layers, rows, columns = sizes
    source = Rows(sizes, pv, base, got_a, got_b)
    lane = lanes_of((SUB, columns))
    from_a = jnp.logical_xor(lax.rem(lane, 4) < 2, is_even("gx"))

    def fields(group):
        block = pl.ds(group * SUB, SUB)
        sides = jnp.where(from_a, side_a[block, :], side_b[block, :])
        value, dx, sx, dx2, sx2 = {}, {}, {}, {}, {}
        for layer in range(layers):
            for row in range(-2, rows + 2):
                here = source.get(layer, row, group)
                value[layer, row] = here
                if row == -2 or row == rows + 1:
                    continue
                place = layer * (rows + 2) + row + 1
                edge = pltpu.roll(sides, (columns - 2 - 4 * place) % columns, 1)
                left, right = jnp.where(lane == columns - 1, edge, here), jnp.where(lane == 0, edge, here)
                west, east = pltpu.roll(left, 1, 1), pltpu.roll(right, columns - 1, 1)
                dx[layer, row], sx[layer, row] = east - west, east + west
                if 0 <= row < rows:
                    left, right = jnp.where(lane >= columns - 2, edge, here), jnp.where(lane < 2, edge, here)
                    west, east = pltpu.roll(left, 2, 1), pltpu.roll(right, columns - 2, 1)
                    dx2[layer, row], sx2[layer, row] = east - west, east + west
        dy, near, near_dx, near_dy = {}, {}, {}, {}
        for layer in range(layers):
            for row in range(rows):
                k = (layer, row)
                up, down = (layer, row - 1), (layer, row + 1)
                dy[k] = value[down] - value[up]
                near[k] = sx[k] + (value[down] + value[up])
                near_dx[k] = dx2[k] + (dx[down] + dx[up])
                near_dy[k] = (sx[down] - sx[up]) + (value[layer, row + 2] - value[layer, row - 2])
        return value, dx, sx, sx2, dy, near, near_dx, near_dy

    other = lambda layer: layers - 1 - layer
    value, dx, sx, sx2, dy, near, near_dx, near_dy = fields(source.groups)
    for layer in range(layers):
        c, c_other = coupling_pair[layer], coupling_pair[other(layer)]
        a = 1.0 / (4.0 + c)
        for row in range(rows):
            k, o = (layer, row), (other(layer), row)
            base_dx, base_dy = dx[k], dy[k]
            pv_dx = near_dx[k] - (4.0 + c) * base_dx + c * dx[o]
            pv_dy = near_dy[k] - (4.0 + c) * base_dy + c * dy[o]
            j = 0.25 * time_step
            coef[layer * rows + row, 0] = j * (base_dy + a * pv_dy)
            coef[layer * rows + row, 1] = -j * (base_dx + a * pv_dx)
            coef[layer * rows + row, 2] = (j * a * a) * pv_dy
            coef[layer * rows + row, 3] = (-j * a * a) * pv_dx
    v = time_step * hyper_visc
    for group in range(source.groups):
        value, dx, sx, sx2, dy, near, near_dx, near_dy = fields(group)
        for layer in range(layers):
            c, c_other = coupling_pair[layer], coupling_pair[other(layer)]
            cross = c * (4.0 + c) / (4.0 + c_other)
            for row in range(rows):
                k, o = (layer, row), (other(layer), row)
                up, down = (layer, row - 1), (layer, row + 1)
                at = layer * rows + row
                diagonal = sx[down] + sx[up]
                far = sx2[k] + (value[layer, row + 2] + value[layer, row - 2])
                result = (1.0 - 20.0 * v) * value[k] + (8.0 * v) * near[k] - (2.0 * v) * diagonal - v * far
                result = result + (coef[at, 0] * dx[k] + coef[at, 1] * dy[k])
                result = result + coef[at, 2] * (near_dx[k] + cross * dx[o])
                result = result + coef[at, 3] * (near_dy[k] + cross * dy[o])
                evolved[pl.ds(group * SUB, SUB), pl.ds(at * columns, columns)] = result
    whole = evolved[...]
    local = lax.dot_general(
        whole, whole, (((1,), (1,)), ((), ())),
        precision=lax.Precision.HIGHEST, preferred_element_type=jnp.float32,
    ) * scale
    gram[...] = jnp.concatenate([local[g * SUB : (g + 1) * SUB] for g in range(source.groups)], axis=1)


def basis_body(sizes, evolved, gram, basis, upper):
    vectors, layers, rows, columns = sizes
    groups = vectors // SUB
    shape = (SUB, columns)
    lane = lanes_of(shape)
    sub = lax.broadcasted_iota(jnp.int32, shape, 0)
    packed = gram[...]
    work = []
    for group in range(groups):
        turned = pltpu.roll(packed, (columns - group * vectors) % columns, 1)
        unit = jnp.where(lane - vectors == sub + group * SUB, 1.0, 0.0)
        work.append(jnp.where(lane < vectors, turned, unit))
    for k in range(vectors):
        home, at = k // SUB, k % SUB
        line = jnp.broadcast_to(work[home][at : at + 1, :], shape)
        pivot = 1.0 / jnp.broadcast_to(line[:, k : k + 1], shape)
        for group in range(home, groups):
            if group == home and at == SUB - 1:
                continue
            factor = jnp.broadcast_to(work[group][:, k : k + 1], shape) * pivot
            if group == home:
                factor = jnp.where(sub > at, factor, 0.0)
            work[group] = work[group] - factor * line
    inverse = []
    for group in range(groups):
        row = sub + group * SUB
        pivot = jnp.sum(jnp.where(lane == row, work[group], 0.0), axis=1, keepdims=True)
        done = work[group] * (1.0 / jnp.sqrt(jnp.broadcast_to(pivot, shape)))
        upper[pl.ds(group * SUB, SUB), :] = jnp.where(lane >= row, done, 0.0)[:, :vectors]
        inverse.append(pltpu.roll(done, columns - vectors, 1)[:, :vectors])
    inverse = jnp.concatenate(inverse, axis=0)
    stride = layers * rows
    for at in range(stride):
        part = jnp.dot(
            inverse, evolved[:, pl.ds(at * columns, columns)],
            precision=lax.Precision.HIGHEST, preferred_element_type=jnp.float32,
        )
        for group in range(groups):
            basis[pl.ds(group * SUB * stride + at, SUB, stride=stride), :] = part[group * SUB : (group + 1) * SUB]


def local(base_stream, tangent_vectors):
    sizes = tangent_vectors.shape
    vectors, layers, rows, columns = sizes
    pv = tangent_vectors.reshape(vectors * layers * rows, columns)
    base = base_stream.reshape(layers * rows, columns)
    f32 = lambda *shape: jax.ShapeDtypeStruct(shape, jnp.float32)

    def call(body, outs, *operands, scratch=()):
        return pl.pallas_call(
            lambda *refs: body(sizes, *refs),
            out_shape=outs,
            in_specs=[VMEM] * len(operands),
            out_specs=[VMEM] * len(outs),
            scratch_shapes=scratch,
            compiler_params=pltpu.CompilerParams(vmem_limit_bytes=8 << 20),
        )(*operands)

    strip = f32(layers * 2 * vectors + SUB, columns)
    row_a, row_b = call(pack_rows_body, [strip, strip], pv, base)
    got_a, got_b = pairings(row_a, row_b, "gy")
    (side,) = call(pack_columns_body, [f32(vectors + SUB, columns)], pv, base, got_a, got_b)
    side_a, side_b = pairings(side, side, "gx")
    cells = layers * rows * columns
    tiles = lax.axis_size("gy") * lax.axis_size("gx")
    scale = 1.0 / (cells * tiles)
    evolved, gram = call(
        lambda sizes, *refs: stencil_body(sizes, scale, *refs),
        [f32(vectors, cells), f32(SUB, vectors * vectors // SUB)],
        pv, base, got_a, got_b, side_a, side_b,
        scratch=[pltpu.VMEM((layers * rows, 4, SUB, columns), jnp.float32)],
    )
    spread = jnp.broadcast_to(gram[None], (tiles,) + gram.shape)
    gram = lax.all_to_all(spread, ("gy", "gx"), 0, 0, tiled=True).sum(0)
    basis, upper = call(
        basis_body, [f32(vectors * layers * rows, columns), f32(vectors, vectors)], evolved, gram
    )
    return basis.reshape(sizes), upper


def solution(mesh):
    return jax.shard_map(
        local,
        mesh=mesh,
        in_specs=(P("ens", "gy", "gx"), P("ens", None, "gy", "gx")),
        out_specs=(P("ens", None, "gy", "gx"), P("ens", None)),
        check_vma=False,
    )
```

time: 135 us -> 33.1 us (0.25)
  other arithmetic: 74.9 us -> 0.02 us
  waiting for transfers between devices: 18.8 us -> 5.54 us
  blocking collectives: 19.4 us -> 11.3 us
  Pallas kernels: 0 us -> 6.46 us
  matrix products: 6.21 us -> 0 us
  local copies, waits for them, and re-layouts: 5.6 us -> 1.65 us
    another operation x50 -> x0, other arithmetic: 60 us -> none  [the longest x45 53.9 us: combine_factors(): return jnp.linalg.cholesky(summed).T]
    all_gather x1 -> x0, blocking collectives: 19.4 us -> none  [combined_all(): pieces = lax.all_gather(value, axis)]
    ppermute x8 -> x4, waiting for transfers between devices: 18.8 us -> 5.54 us  [the longest x2 5.54 us: pairings(): lax.ppermute(value_b, axis, [(i, (i + 1 if i % 2 else i - 1) % count) for...]
    all_to_all x0 -> x1, blocking collectives: none -> 11.3 us  [local(): gram = lax.all_to_all(spread, ('gy', 'gx'), 0, 0, tiled=True).sum(0)]
    transpose x16 -> x0, other arithmetic: 10.4 us -> none  [the longest x15 9.74 us: combine_factors(): return jnp.linalg.cholesky(summed).T]
    pallas_call x0 -> x4, Pallas kernels: none -> 6.46 us  [call(): pl.pallas_call(lambda *refs: body(sizes, *refs), out_shape=outs, in_specs...]
    dot_general x31 -> x0, matrix products: 5.8 us -> none  [the longest x15 3.24 us: combine_factors(): jnp.dot(right_factor.T, right_factor, precision=lax.Precision.HIGHEST, pr...]
    div x18 -> x0, other arithmetic: 3.19 us -> none  [the longest x1 2.3 us: padded_relax(): (padded_neighbours(stream_ext) + coupling * jnp.flip(inner_part(stream_ex...]
  transfers between devices with their start and end apart: 8 -> 4, of which waited for: 5 -> 2; matrix products, arithmetic and copies ran while one was open for 1% -> 0% of each run, Pallas kernels for 0% -> 0%
where the time goes in v1:
time: 33.1 us; the launch traced here: 32.8 us
  blocking collectives  11.3 us (34%)
  starting transfers between devices  7.26 us (22%)
  Pallas kernels  6.46 us (20%)
  waiting for transfers between devices  5.54 us (17%)
  local copies, waits for them, and re-layouts  1.65 us (5%)
  between operations  0.65 us (2%)
    all_to_all x1, blocking collectives, local(): gram = lax.all_to_all(spread, ('gy', 'gx'), 0, 0, tiled=True).sum(0)  11.3 us
    pallas_call x4, Pallas kernels, call(): pl.pallas_call(lambda *refs: body(sizes, *refs), out_shape=outs, in_specs...  6.46 us
    ppermute x2, waiting for transfers between devices, pairings(): lax.ppermute(value_b, axis, [(i, (i + 1 if i % 2 else i - 1) % count) for...  5.54 us
    ppermute x2, starting transfers between devices, pairings(): lax.ppermute(value_a, axis, [(i, (i + 1 if i % 2 == 0 else i - 1) % count...  4.68 us
    ppermute x2, starting transfers between devices, pairings(): lax.ppermute(value_b, axis, [(i, (i + 1 if i % 2 else i - 1) % count) for...  2.58 us
    unnamed x4, local copies, waits for them, and re-layouts  1.64 us
  transfers between devices with their start and end apart: 4, of which 2 were waited for; matrix products, arithmetic and copies ran while one was open for 0% of the time, Pallas kernels for 0%

profile of v1, /device:TPU:0, one launch (start us, length us, event | category | flops | bytes accessed | tf_op | source)
XLA Modules:
  0.0 32.8 jit_solution(4915777451896298461)
XLA Ops:
  0.6 0.0 copy-start
  0.6 0.9 %copy-done = f32[32,2,8,128]{3,2,1,0:T(8,128)S(1)} copy-done((f32[32,2,8,128]{3,2,1,0:T(8,128)S(1)}, f32[32,2,8,128]{3,2,1,0:T(8,128)}, u32[]{:S(2)}) %copy-start) | copy-done | bytes 262168
  1.6 0.0 copy-start.1
  1.6 0.7 %copy-done.1 = f32[2,8,128]{2,1,0:T(8,128)S(1)} copy-done((f32[2,8,128]{2,1,0:T(8,128)S(1)}, f32[2,8,128]{2,1,0:T(8,128)}, u32[]{:S(2)}) %copy-start.1) | copy-done | bytes 8216
  2.3 3.1 %collective-permute-start = (f32[136,128]{1,0:T(8,128)S(1)}, f32[136,128]{1,0:T(8,128)S(1)}, u32[]{:S(2)}, u32[]{:S(2)}) collective-permute-start(f32[136,128]{1,0:T(8,128)S(1)} %get-tuple-element.8), channel_id=1, source_target_pairs={{0,4},{4,0},{8,12},{12,8},{1,5},{5,1},{9,13},{13,9},{2,6},{6,2},{1... | collective-permute-start | bytes 208904 | tf_op jit(solution)/shard_map/ppermute | solution.py:19
  5.4 2.5 %collective-permute-start.1 = (f32[136,128]{1,0:T(8,128)S(1)}, f32[136,128]{1,0:T(8,128)S(1)}, u32[]{:S(2)}, u32[]{:S(2)}) collective-permute-start(f32[136,128]{1,0:T(8,128)S(1)} %get-tuple-element.9), channel_id=1, source_target_pairs={{0,12},{4,8},{8,4},{12,0},{1,13},{5,9},{9,5},{13,1},{2,14},{6,10},... | collective-permute-start | bytes 208904 | tf_op jit(solution)/shard_map/ppermute | solution.py:18
  7.9 0.0 collective-permute-done.refs_2_
  7.9 3.8 %collective-permute-done.1.refs_3_ = f32[136,128]{1,0:T(8,128)S(1)} collective-permute-done((f32[136,128]{1,0:T(8,128)S(1)}, f32[136,128]{1,0:T(8,128)S(1)}, u32[]{:S(2)}, u32[]{:S(2)}) %collective-permute-start.1) | collective-permute-done | bytes 69664 | tf_op jit(solution)/shard_map/ppermute | solution.py:18
  11.7 0.2 shard_map.42
  11.9 0.1 collective-permute-start.3
  12.0 1.6 %collective-permute-start.2 = (f32[40,128]{1,0:T(8,128)S(1)}, f32[40,128]{1,0:T(8,128)S(1)}, u32[]{:S(2)}, u32[]{:S(2)}) collective-permute-start(f32[40,128]{1,0:T(8,128)S(1)} %shard_map.42), channel_id=1, source_target_pairs={{0,1},{1,0},{2,3},{3,2},{4,5},{5,4},{6,7},{7,6},{8,9},{9,8},{10,11... | collective-permute-start | bytes 61448 | tf_op jit(solution)/shard_map/ppermute | solution.py:19
  13.6 1.8 %collective-permute-done.3.refs_5_ = f32[40,128]{1,0:T(8,128)S(1)} collective-permute-done((f32[40,128]{1,0:T(8,128)S(1)}, f32[40,128]{1,0:T(8,128)S(1)}, u32[]{:S(2)}, u32[]{:S(2)}) %collective-permute-start.3) | collective-permute-done | bytes 20512 | tf_op jit(solution)/shard_map/ppermute | solution.py:18
  15.3 0.0 collective-permute-done.2.refs_4_
  15.3 1.1 %shard_map.43 = (f32[32,2048]{1,0:T(8,128)S(1)}, f32[8,128]{1,0:T(8,128)S(1)}) custom-call(f32[512,128]{1,0:T(8,128)S(1)} %bitcast.5, f32[16,128]{1,0:T(8,128)S(1)} %bitcast.8, f32[136,128]{1,0:T(8,128)S(1)} %collective-permute-done.refs_2_, f32[136,128]{1,0:T(8,128)S(1)} %collective-permute-done.1.refs_3_, f32[40,128]{1,0:T(8,128)S(1)} %collective-permute-done.2.refs_4_, ...), custom_call_target="tpu_custom_call" | custom-call | tf_op jit(solution)/shard_map/pallas_call | solution.py:220
  16.4 11.3 %all_to_all.5 = f32[16,8,128]{2,1,0:T(8,128)S(1)} all-to-all(f32[16,8,128]{2,1,0:T(8,128)S(1)} %broadcast_in_dim.2), channel_id=1, replica_groups=mesh['ens'=2,'gy'=4,'gx'=4] {'gy','gx'}, dimensions={0} | all-to-all | bytes 131072 | tf_op jit(solution)/shard_map/all_to_all | solution.py:244
  27.7 5.1 %shard_map.44 = (f32[512,128]{1,0:T(8,128)}, f32[32,32]{1,0:T(8,128)}) custom-call(f32[32,2048]{1,0:T(8,128)S(1)} %get-tuple-element.10.refs_0_, f32[8,128]{1,0:T(8,128)S(1)} %reduce_sum.9.refs_1_), custom_call_target="tpu_custom_call" | custom-call | tf_op jit(solution)/shard_map/pallas_call | solution.py:220
  (3 shorter events, 0.1 us)
Async XLA Ops:
  0.6 1.0 %copy-start = (f32[32,2,8,128]{3,2,1,0:T(8,128)S(1)}, f32[32,2,8,128]{3,2,1,0:T(8,128)}, u32[]{:S(2)}) copy-start(f32[32,2,8,128]{3,2,1,0:T(8,128)} %param.3) | copy-start | bytes 786436
  1.6 0.7 %copy-start.1 = (f32[2,8,128]{2,1,0:T(8,128)S(1)}, f32[2,8,128]{2,1,0:T(8,128)}, u32[]{:S(2)}) copy-start(f32[2,8,128]{2,1,0:T(8,128)} %param.2) | copy-start | bytes 24580
  2.3 5.6 %collective-permute-start = (f32[136,128]{1,0:T(8,128)S(1)}, f32[136,128]{1,0:T(8,128)S(1)}, u32[]{:S(2)}, u32[]{:S(2)}) collective-permute-start(f32[136,128]{1,0:T(8,128)S(1)} %get-tuple-element.8), channel_id=1, source_target_pairs={{0,4},{4,0},{8,12},{12,8},{1,5},{5,1},{9,13},{13,9},{2,6},{6,2},{1... | collective-permute-start | bytes 208904 | tf_op jit(solution)/shard_map/ppermute | solution.py:19
  5.4 6.2 %collective-permute-start.1 = (f32[136,128]{1,0:T(8,128)S(1)}, f32[136,128]{1,0:T(8,128)S(1)}, u32[]{:S(2)}, u32[]{:S(2)}) collective-permute-start(f32[136,128]{1,0:T(8,128)S(1)} %get-tuple-element.9), channel_id=1, source_target_pairs={{0,12},{4,8},{8,4},{12,0},{1,13},{5,9},{9,5},{13,1},{2,14},{6,10},... | collective-permute-start | bytes 208904 | tf_op jit(solution)/shard_map/ppermute | solution.py:18
  11.9 3.4 %collective-permute-start.3 = (f32[40,128]{1,0:T(8,128)S(1)}, f32[40,128]{1,0:T(8,128)S(1)}, u32[]{:S(2)}, u32[]{:S(2)}) collective-permute-start(f32[40,128]{1,0:T(8,128)S(1)} %shard_map.42), channel_id=1, source_target_pairs={{0,3},{1,2},{2,1},{3,0},{4,7},{5,6},{6,5},{7,4},{8,11},{9,10},{10,... | collective-permute-start | bytes 61448 | tf_op jit(solution)/shard_map/ppermute | solution.py:18
  12.0 3.3 %collective-permute-start.2 = (f32[40,128]{1,0:T(8,128)S(1)}, f32[40,128]{1,0:T(8,128)S(1)}, u32[]{:S(2)}, u32[]{:S(2)}) collective-permute-start(f32[40,128]{1,0:T(8,128)S(1)} %shard_map.42), channel_id=1, source_target_pairs={{0,1},{1,0},{2,3},{3,2},{4,5},{5,4},{6,7},{7,6},{8,9},{9,8},{10,11... | collective-permute-start | bytes 61448 | tf_op jit(solution)/shard_map/ppermute | solution.py:19

commit v2 on v1

--- a/solution.py
+++ b/solution.py
@@ -58,9 +58,19 @@
         return self.own(layer, row, group)
 
 
-def pack_rows_body(sizes, pv, base, out_a, out_b):
-    vectors, layers, rows, columns = sizes
-    source = Rows(sizes, pv, base, None, None)
+def pack_rows_body(sizes, pv, base, out_a, out_b, pv_rows, base_rows, done):
+    vectors, layers, rows, columns = sizes
+    ends = (0, rows - 2)
+    copies = [
+        pltpu.make_async_copy(pv.at[:, pl.ds(first, 2), :], pv_rows.at[:, pl.ds(first, 2), :], done.at[n])
+        for n, first in enumerate(ends)
+    ]
+    copies.append(pltpu.make_async_copy(base, base_rows, done.at[2]))
+    for copy in copies:
+        copy.start()
+    for copy in copies:
+        copy.wait()
+    source = Rows(sizes, pv_rows.reshape(vectors * layers * rows, columns), base_rows, None, None)
     for layer in range(layers):
         for step in range(2):
             for group in range(source.groups + 1):
@@ -180,17 +190,29 @@
         turned = pltpu.roll(packed, (columns - group * vectors) % columns, 1)
         unit = jnp.where(lane - vectors == sub + group * SUB, 1.0, 0.0)
         work.append(jnp.where(lane < vectors, turned, unit))
-    for k in range(vectors):
-        home, at = k // SUB, k % SUB
-        line = jnp.broadcast_to(work[home][at : at + 1, :], shape)
-        pivot = 1.0 / jnp.broadcast_to(line[:, k : k + 1], shape)
-        for group in range(home, groups):
-            if group == home and at == SUB - 1:
-                continue
-            factor = jnp.broadcast_to(work[group][:, k : k + 1], shape) * pivot
-            if group == home:
-                factor = jnp.where(sub > at, factor, 0.0)
-            work[group] = work[group] - factor * line
+    for home in range(groups):
+        first = home * SUB
+        column = {
+            (group, j): jnp.broadcast_to(work[group][:, first + j : first + j + 1], shape)
+            for group in range(home, groups)
+            for j in range(SUB)
+        }
+        for at in range(SUB):
+            inverse_pivot = jnp.broadcast_to((1.0 / column[home, at])[at : at + 1, :], shape)
+            line = jnp.broadcast_to(work[home][at : at + 1, :], shape)
+            for group in range(home, groups):
+                factor = column[group, at] * inverse_pivot
+                if group == home:
+                    factor = jnp.where(sub > at, factor, 0.0)
+                for j in range(at + 1, SUB):
+                    level = jnp.broadcast_to(column[home, j][at : at + 1, :], shape)
+                    if group == home:
+                        column[home, j, "next"] = column[home, j] - factor * level
+                    else:
+                        column[group, j] = column[group, j] - factor * level
+                work[group] = work[group] - factor * line
+            for j in range(at + 1, SUB):
+                column[home, j] = column.pop((home, j, "next"))
     inverse = []
     for group in range(groups):
         row = sub + group * SUB
@@ -200,13 +222,16 @@
         inverse.append(pltpu.roll(done, columns - vectors, 1)[:, :vectors])
     inverse = jnp.concatenate(inverse, axis=0)
     stride = layers * rows
-    for at in range(stride):
+    wide = 2 if stride % 2 == 0 else 1
+    for first in range(0, stride, wide):
         part = jnp.dot(
-            inverse, evolved[:, pl.ds(at * columns, columns)],
+            inverse, evolved[:, pl.ds(first * columns, wide * columns)],
             precision=lax.Precision.HIGHEST, preferred_element_type=jnp.float32,
         )
-        for group in range(groups):
-            basis[pl.ds(group * SUB * stride + at, SUB, stride=stride), :] = part[group * SUB : (group + 1) * SUB]
+        for n in range(wide):
+            for group in range(groups):
+                at = pl.ds(group * SUB * stride + first + n, SUB, stride=stride)
+                basis[at, :] = part[group * SUB : (group + 1) * SUB, n * columns : (n + 1) * columns]
 
 
 def local(base_stream, tangent_vectors):
@@ -216,18 +241,28 @@
     base = base_stream.reshape(layers * rows, columns)
     f32 = lambda *shape: jax.ShapeDtypeStruct(shape, jnp.float32)
 
-    def call(body, outs, *operands, scratch=()):
+    def call(body, outs, *operands, scratch=(), inputs=VMEM):
         return pl.pallas_call(
             lambda *refs: body(sizes, *refs),
             out_shape=outs,
-            in_specs=[VMEM] * len(operands),
+            in_specs=[inputs] * len(operands),
             out_specs=[VMEM] * len(outs),
             scratch_shapes=scratch,
             compiler_params=pltpu.CompilerParams(vmem_limit_bytes=8 << 20),
         )(*operands)
 
     strip = f32(layers * 2 * vectors + SUB, columns)
-    row_a, row_b = call(pack_rows_body, [strip, strip], pv, base)
+    row_a, row_b = call(
+        pack_rows_body, [strip, strip],
+        pltpu.with_memory_space_constraint(tangent_vectors.reshape(vectors * layers, rows, columns), pltpu.HBM),
+        pltpu.with_memory_space_constraint(base, pltpu.HBM),
+        inputs=pl.BlockSpec(memory_space=pltpu.HBM),
+        scratch=[
+            pltpu.VMEM((vectors * layers, rows, columns), jnp.float32),
+            pltpu.VMEM((layers * rows, columns), jnp.float32),
+            pltpu.SemaphoreType.DMA((3,)),
+        ],
+    )
     got_a, got_b = pairings(row_a, row_b, "gy")
     (side,) = call(pack_columns_body, [f32(vectors + SUB, columns)], pv, base, got_a, got_b)
     side_a, side_b = pairings(side, side, "gx")

time: 33.1 us -> 29.2 us (0.88)
  Pallas kernels: 6.46 us -> 4.28 us
  local copies, waits for them, and re-layouts: 1.65 us -> 0.02 us
    pallas_call x4, Pallas kernels: 6.46 us -> 4.28 us  [call(): pl.pallas_call(lambda *refs: body(sizes, *refs), out_shape=outs, in_specs...]
    unnamed x4, local copies, waits for them, and re-layouts: 1.64 us -> 0.01 us
where the time goes in v2:
time: 29.2 us; the launch traced here: 29 us
  blocking collectives  11.2 us (38%)
  starting transfers between devices  7.26 us (25%)
  waiting for transfers between devices  5.54 us (19%)
  Pallas kernels  4.28 us (15%)
  between operations  0.67 us (2%)
    all_to_all x1, blocking collectives, local(): gram = lax.all_to_all(spread, ('gy', 'gx'), 0, 0, tiled=True).sum(0)  11.2 us
    ppermute x2, waiting for transfers between devices, pairings(): lax.ppermute(value_b, axis, [(i, (i + 1 if i % 2 else i - 1) % count) for...  5.54 us
    ppermute x2, starting transfers between devices, pairings(): lax.ppermute(value_a, axis, [(i, (i + 1 if i % 2 == 0 else i - 1) % count...  4.68 us
    pallas_call x4, Pallas kernels, call(): pl.pallas_call(lambda *refs: body(sizes, *refs), out_shape=outs, in_specs...  4.28 us
    ppermute x2, starting transfers between devices, pairings(): lax.ppermute(value_b, axis, [(i, (i + 1 if i % 2 else i - 1) % count) for...  2.58 us
  transfers between devices with their start and end apart: 4, of which 2 were waited for; matrix products, arithmetic and copies ran while one was open for 0% of the time, Pallas kernels for 0%

profile of v2, /device:TPU:0, one launch (start us, length us, event | category | flops | bytes accessed | tf_op | source)
XLA Modules:
  0.0 29.0 jit_solution(14996667484991636445)
XLA Ops:
  0.6 0.0 copy-start
  0.6 0.0 copy-start.1
  0.6 1.0 %shard_map.41 = (f32[136,128]{1,0:T(8,128)S(1)}, f32[136,128]{1,0:T(8,128)S(1)}) custom-call(f32[64,8,128]{2,1,0:T(8,128)} %bitcast.4, f32[16,128]{1,0:T(8,128)} %bitcast.7), custom_call_target="tpu_custom_call" | custom-call | tf_op jit(solution)/shard_map/pallas_call | solution.py:245
  1.6 3.1 %collective-permute-start = (f32[136,128]{1,0:T(8,128)S(1)}, f32[136,128]{1,0:T(8,128)S(1)}, u32[]{:S(2)}, u32[]{:S(2)}) collective-permute-start(f32[136,128]{1,0:T(8,128)S(1)} %get-tuple-element.8), channel_id=1, source_target_pairs={{0,4},{4,0},{8,12},{12,8},{1,5},{5,1},{9,13},{13,9},{2,6},{6,2},{1... | collective-permute-start | bytes 208904 | tf_op jit(solution)/shard_map/ppermute | solution.py:19
  4.8 2.5 %collective-permute-start.1 = (f32[136,128]{1,0:T(8,128)S(1)}, f32[136,128]{1,0:T(8,128)S(1)}, u32[]{:S(2)}, u32[]{:S(2)}) collective-permute-start(f32[136,128]{1,0:T(8,128)S(1)} %get-tuple-element.9), channel_id=1, source_target_pairs={{0,12},{4,8},{8,4},{12,0},{1,13},{5,9},{9,5},{13,1},{2,14},{6,10},... | collective-permute-start | bytes 208904 | tf_op jit(solution)/shard_map/ppermute | solution.py:18
  7.2 0.0 collective-permute-done.refs_2_
  7.2 3.8 %collective-permute-done.1.refs_3_ = f32[136,128]{1,0:T(8,128)S(1)} collective-permute-done((f32[136,128]{1,0:T(8,128)S(1)}, f32[136,128]{1,0:T(8,128)S(1)}, u32[]{:S(2)}, u32[]{:S(2)}) %collective-permute-start.1) | collective-permute-done | bytes 69664 | tf_op jit(solution)/shard_map/ppermute | solution.py:18
  11.0 0.0 copy-done
  11.0 0.0 copy-done.1
  11.0 0.2 shard_map.42
  11.2 0.1 collective-permute-start.3
  11.3 1.6 %collective-permute-start.2 = (f32[40,128]{1,0:T(8,128)S(1)}, f32[40,128]{1,0:T(8,128)S(1)}, u32[]{:S(2)}, u32[]{:S(2)}) collective-permute-start(f32[40,128]{1,0:T(8,128)S(1)} %shard_map.42), channel_id=1, source_target_pairs={{0,1},{1,0},{2,3},{3,2},{4,5},{5,4},{6,7},{7,6},{8,9},{9,8},{10,11... | collective-permute-start | bytes 61448 | tf_op jit(solution)/shard_map/ppermute | solution.py:19
  12.9 1.8 %collective-permute-done.3.refs_5_ = f32[40,128]{1,0:T(8,128)S(1)} collective-permute-done((f32[40,128]{1,0:T(8,128)S(1)}, f32[40,128]{1,0:T(8,128)S(1)}, u32[]{:S(2)}, u32[]{:S(2)}) %collective-permute-start.3) | collective-permute-done | bytes 20512 | tf_op jit(solution)/shard_map/ppermute | solution.py:18
  14.7 0.0 collective-permute-done.2.refs_4_
  14.7 1.1 %shard_map.43 = (f32[32,2048]{1,0:T(8,128)S(1)}, f32[8,128]{1,0:T(8,128)S(1)}) custom-call(f32[512,128]{1,0:T(8,128)S(1)} %bitcast.6, f32[16,128]{1,0:T(8,128)S(1)} %bitcast.9, f32[136,128]{1,0:T(8,128)S(1)} %collective-permute-done.refs_2_, f32[136,128]{1,0:T(8,128)S(1)} %collective-permute-done.1.refs_3_, f32[40,128]{1,0:T(8,128)S(1)} %collective-permute-done.2.refs_4_, ...), custom_call_target="tpu_custom_call" | custom-call | tf_op jit(solution)/shard_map/pallas_call | solution.py:245
  15.8 11.2 %all_to_all.5 = f32[16,8,128]{2,1,0:T(8,128)S(1)} all-to-all(f32[16,8,128]{2,1,0:T(8,128)S(1)} %broadcast_in_dim.2), channel_id=1, replica_groups=mesh['ens'=2,'gy'=4,'gx'=4] {'gy','gx'}, dimensions={0} | all-to-all | bytes 131072 | tf_op jit(solution)/shard_map/all_to_all | solution.py:279
  27.1 2.0 %shard_map.44 = (f32[512,128]{1,0:T(8,128)}, f32[32,32]{1,0:T(8,128)}) custom-call(f32[32,2048]{1,0:T(8,128)S(1)} %get-tuple-element.10.refs_0_, f32[8,128]{1,0:T(8,128)S(1)} %reduce_sum.9.refs_1_), custom_call_target="tpu_custom_call" | custom-call | tf_op jit(solution)/shard_map/pallas_call | solution.py:245
  (2 shorter events, 0.0 us)
Async XLA Ops:
  0.6 10.4 %copy-start = (f32[32,2,8,128]{3,2,1,0:T(8,128)S(1)}, f32[32,2,8,128]{3,2,1,0:T(8,128)}, u32[]{:S(2)}) copy-start(f32[32,2,8,128]{3,2,1,0:T(8,128)} %param.3) | copy-start | bytes 786436
  0.6 10.4 %copy-start.1 = (f32[2,8,128]{2,1,0:T(8,128)S(1)}, f32[2,8,128]{2,1,0:T(8,128)}, u32[]{:S(2)}) copy-start(f32[2,8,128]{2,1,0:T(8,128)} %param.2) | copy-start | bytes 24580
  1.6 5.6 %collective-permute-start = (f32[136,128]{1,0:T(8,128)S(1)}, f32[136,128]{1,0:T(8,128)S(1)}, u32[]{:S(2)}, u32[]{:S(2)}) collective-permute-start(f32[136,128]{1,0:T(8,128)S(1)} %get-tuple-element.8), channel_id=1, source_target_pairs={{0,4},{4,0},{8,12},{12,8},{1,5},{5,1},{9,13},{13,9},{2,6},{6,2},{1... | collective-permute-start | bytes 208904 | tf_op jit(solution)/shard_map/ppermute | solution.py:19
  4.8 6.2 %collective-permute-start.1 = (f32[136,128]{1,0:T(8,128)S(1)}, f32[136,128]{1,0:T(8,128)S(1)}, u32[]{:S(2)}, u32[]{:S(2)}) collective-permute-start(f32[136,128]{1,0:T(8,128)S(1)} %get-tuple-element.9), channel_id=1, source_target_pairs={{0,12},{4,8},{8,4},{12,0},{1,13},{5,9},{9,5},{13,1},{2,14},{6,10},... | collective-permute-start | bytes 208904 | tf_op jit(solution)/shard_map/ppermute | solution.py:18
  11.2 3.4 %collective-permute-start.3 = (f32[40,128]{1,0:T(8,128)S(1)}, f32[40,128]{1,0:T(8,128)S(1)}, u32[]{:S(2)}, u32[]{:S(2)}) collective-permute-start(f32[40,128]{1,0:T(8,128)S(1)} %shard_map.42), channel_id=1, source_target_pairs={{0,3},{1,2},{2,1},{3,0},{4,7},{5,6},{6,5},{7,4},{8,11},{9,10},{10,... | collective-permute-start | bytes 61448 | tf_op jit(solution)/shard_map/ppermute | solution.py:18
  11.3 3.3 %collective-permute-start.2 = (f32[40,128]{1,0:T(8,128)S(1)}, f32[40,128]{1,0:T(8,128)S(1)}, u32[]{:S(2)}, u32[]{:S(2)}) collective-permute-start(f32[40,128]{1,0:T(8,128)S(1)} %shard_map.42), channel_id=1, source_target_pairs={{0,1},{1,0},{2,3},{3,2},{4,5},{5,4},{6,7},{7,6},{8,9},{9,8},{10,11... | collective-permute-start | bytes 61448 | tf_op jit(solution)/shard_map/ppermute | solution.py:19

commit v3 on v2

v3 whole, which is shorter than its diff:
```python
import jax
import jax.numpy as jnp
from jax import lax
from jax.experimental import pallas as pl
from jax.experimental.pallas import tpu as pltpu
from jax.sharding import PartitionSpec as P

coupling_pair = (0.6, 0.3)
time_step = 0.05
hyper_visc = 0.1

SUB = 8
EDGE = 4
SPAN = 2 * EDGE
VMEM = pl.BlockSpec(memory_space=pltpu.VMEM)


def lanes_of(shape):
    return lax.broadcasted_iota(jnp.int32, shape, len(shape) - 1)


class Rows:
    def __init__(self, sizes, pv, base, above, below):
        self.vectors, self.layers, self.rows, self.columns = sizes
        self.groups = self.vectors // SUB
        self.pv, self.base, self.above, self.below = pv, base, above, below

    def halo(self, strip, layer, step, group):
        if group < self.groups:
            return strip[pl.ds((layer * 2 + step) * self.vectors + group * SUB, SUB), :]
        found = strip[pl.ds(self.layers * 2 * self.vectors + layer * 2 + step, 1), :]
        return jnp.broadcast_to(found, (SUB, self.columns))

    def own(self, layer, row, group):
        if group < self.groups:
            stride = self.layers * self.rows
            return self.pv[pl.ds(group * SUB * stride + layer * self.rows + row, SUB, stride=stride), :]
        return jnp.broadcast_to(self.base[pl.ds(layer * self.rows + row, 1), :], (SUB, self.columns))

    def get(self, layer, row, group):
        if row < 0:
            return self.halo(self.above, layer, row + 2, group)
        if row >= self.rows:
            return self.halo(self.below, layer, row - self.rows, group)
        return self.own(layer, row, group)


def pack_rows_body(sizes, pv, base, bottom, top, pv_rows, base_rows, done):
    vectors, layers, rows, columns = sizes
    ends = (0, rows - 2)
    copies = [
        pltpu.make_async_copy(pv.at[:, pl.ds(first, 2), :], pv_rows.at[:, pl.ds(first, 2), :], done.at[n])
        for n, first in enumerate(ends)
    ]
    copies.append(pltpu.make_async_copy(base, base_rows, done.at[2]))
    for copy in copies:
        copy.start()
    for copy in copies:
        copy.wait()
    source = Rows(sizes, pv_rows.reshape(vectors * layers * rows, columns), base_rows, None, None)
    for out, first in ((top, 0), (bottom, rows - 2)):
        for layer in range(layers):
            for step in range(2):
                for group in range(source.groups):
                    at = pl.ds((layer * 2 + step) * vectors + group * SUB, SUB)
                    out[at, :] = source.own(layer, first + step, group)
                at = pl.ds(layers * 2 * vectors + layer * 2 + step, 1)
                out[at, :] = source.own(layer, first + step, source.groups)[:1]
        out[pl.ds(layers * 2 * (vectors + 1), SUB - layers * 2), :] = jnp.zeros((SUB - layers * 2, columns), jnp.float32)


class Fields:
    pass


def base_weights(at, other, layer):
    c = coupling_pair[layer]
    a = 1.0 / (4.0 + c)
    j = 0.25 * time_step
    pv_dx = at.near_dx - (4.0 + c) * at.dx + c * other.dx
    pv_dy = at.near_dy - (4.0 + c) * at.dy + c * other.dy
    return (
        j * (at.dy + a * pv_dy),
        -j * (at.dx + a * pv_dx),
        (j * a * a) * pv_dy,
        (-j * a * a) * pv_dx,
    )


def stepped(at, other, layer, weights):
    c, c_other = coupling_pair[layer], coupling_pair[1 - layer]
    cross = c * (4.0 + c) / (4.0 + c_other)
    v = time_step * hyper_visc
    result = (1.0 - 20.0 * v) * at.value + (8.0 * v) * at.near - (2.0 * v) * at.diagonal - v * at.far
    result = result + (weights[0] * at.dx + weights[1] * at.dy)
    result = result + weights[2] * (at.near_dx + cross * other.dx)
    return result + weights[3] * (at.near_dy + cross * other.dy)


def packed_gram(whole, scale):
    local = lax.dot_general(
        whole, whole, (((1,), (1,)), ((), ())),
        precision=lax.Precision.HIGHEST, preferred_element_type=jnp.float32,
    ) * scale
    return jnp.concatenate([local[at : at + SUB] for at in range(0, whole.shape[0], SUB)], axis=1)


def stencil_body(sizes, scale, pv, base, above, below, evolved, message, coef):
    vectors, layers, rows, columns = sizes
    source = Rows(sizes, pv, base, above, below)
    lane = lanes_of((SUB, columns))
    inside = jnp.logical_and(lane >= 2, lane < columns - 2)
    place = lane // SPAN

    def fields(group):
        value, dx, sx, dx2, sx2 = {}, {}, {}, {}, {}
        for layer in range(layers):
            edges = jnp.zeros((SUB, columns), jnp.float32)
            for row in range(-2, rows + 2):
                here = source.get(layer, row, group)
                value[layer, row] = here
                turned = pltpu.roll(here, (EDGE + SPAN * (row + 2)) % columns, 1)
                edges = jnp.where(place == row + 2, turned, edges)
                if row == -2 or row == rows + 1:
                    continue
                west, east = pltpu.roll(here, 1, 1), pltpu.roll(here, columns - 1, 1)
                dx[layer, row], sx[layer, row] = east - west, east + west
                if 0 <= row < rows:
                    west, east = pltpu.roll(here, 2, 1), pltpu.roll(here, columns - 2, 1)
                    dx2[layer, row], sx2[layer, row] = east - west, east + west
            message[pl.ds(SUB + layer * (vectors + SUB) + group * SUB, SUB), :] = edges
        found = {}
        for layer in range(layers):
            for row in range(rows):
                up, down = (layer, row - 1), (layer, row + 1)
                at = found[layer, row] = Fields()
                at.value, at.dx = value[layer, row], dx[layer, row]
                at.dy = value[down] - value[up]
                at.near = sx[layer, row] + (value[down] + value[up])
                at.near_dx = dx2[layer, row] + (dx[down] + dx[up])
                at.near_dy = (sx[down] - sx[up]) + (value[layer, row + 2] - value[layer, row - 2])
                at.diagonal = sx[down] + sx[up]
                at.far = sx2[layer, row] + (value[layer, row + 2] + value[layer, row - 2])
        return found

    found = fields(source.groups)
    for layer in range(layers):
        for row in range(rows):
            for n, weight in enumerate(base_weights(found[layer, row], found[1 - layer, row], layer)):
                coef[layer * rows + row, n] = weight
    for group in range(source.groups):
        found = fields(group)
        for layer in range(layers):
            for row in range(rows):
                at = layer * rows + row
                weights = [coef[at, n] for n in range(4)]
                result = stepped(found[layer, row], found[1 - layer, row], layer, weights)
                evolved[pl.ds(group * SUB, SUB), pl.ds(at * columns, columns)] = jnp.where(inside, result, 0.0)
    message[pl.ds(0, SUB), :] = packed_gram(evolved[...], scale)


def strip_fields(here, columns):
    turn = lambda value, by: pltpu.roll(value, by % columns, 1)
    at = Fields()
    west, east = turn(here, 1), turn(here, -1)
    at.value, at.dx, sx = here, east - west, east + west
    west, east = turn(here, 2), turn(here, -2)
    dx2, sx2 = east - west, east + west
    up, down = turn(here, SPAN), turn(here, -SPAN)
    at.dy, at.near = down - up, sx + (down + up)
    at.near_dx = dx2 + (turn(at.dx, -SPAN) + turn(at.dx, SPAN))
    far_up, far_down = turn(here, 2 * SPAN), turn(here, -2 * SPAN)
    sx_up, sx_down = turn(sx, SPAN), turn(sx, -SPAN)
    at.near_dy = (sx_down - sx_up) + (far_down - far_up)
    at.diagonal, at.far = sx_down + sx_up, sx2 + (far_down + far_up)
    return at


def join_body(sizes, scale, half, last, *refs):
    vectors, layers, rows, columns = sizes
    refs = list(refs)
    mine, got = refs[:2]
    sides_in = refs[2] if half > 1 else None
    outs = refs[3:] if half > 1 else refs[2:]
    message, sides, strips = outs
    groups = vectors // SUB
    shape = (SUB, columns)
    lane = lanes_of(shape)
    column = lax.rem(lane, SPAN)
    west_half = column < EDGE
    valid = jnp.logical_and(
        jnp.logical_and(column >= 2, column < SPAN - 2),
        jnp.logical_and(lane >= 2 * SPAN, lane < (rows + 2) * SPAN),
    )
    tile = lax.axis_index("gx")
    spot = lax.rem(tile, 2 * half)
    first = spot < half
    mid_mine = jnp.logical_xor(west_half, jnp.logical_not(first))
    keep_mid = jnp.logical_or(jnp.logical_and(west_half, spot == half - 1), jnp.logical_and(~west_half, spot == half))
    keep_wrap = jnp.logical_or(jnp.logical_and(west_half, spot == 2 * half - 1), jnp.logical_and(~west_half, spot == 0))
    kinds = (False, True) if last else (False,)
    weights = {}
    for group in (groups, *range(groups)):
        found = {}
        for layer in range(layers):
            at = pl.ds(SUB + layer * (vectors + SUB) + group * SUB, SUB)
            here, there = mine[at, :], got[at, :]
            mid, outer = jnp.where(mid_mine, here, there), jnp.where(mid_mine, there, here)
            if not last:
                message[at, :] = outer
            found[layer, False] = strip_fields(mid, columns)
            if last:
                found[layer, True] = strip_fields(outer, columns)
        for layer in range(layers):
            own = None
            for wrap in kinds:
                at, other = found[layer, wrap], found[1 - layer, wrap]
                if group == groups:
                    weights[layer, wrap] = base_weights(at, other, layer)
                    continue
                result = jnp.where(valid, stepped(at, other, layer, weights[layer, wrap]), 0.0)
                strips[pl.ds(group * SUB, SUB), pl.ds((layer * len(kinds) + wrap) * columns, columns)] = result
                where = pl.ds(layer * vectors + group * SUB, SUB)
                if own is None:
                    own = sides_in[where, :] if half > 1 else jnp.zeros(shape, jnp.float32)
                own = jnp.where(keep_wrap if wrap else keep_mid, result, own)
                if wrap == last:
                    sides[where, :] = own
    head = pl.ds(0, SUB)
    message[head, :] = (mine[head, :] + got[head, :]) + packed_gram(strips[...], scale)


def basis_body(sizes, evolved, sides, gram, basis, upper):
    vectors, layers, rows, columns = sizes
    groups = vectors // SUB
    shape = (SUB, columns)
    lane = lanes_of(shape)
    sub = lax.broadcasted_iota(jnp.int32, shape, 0)
    packed = gram[...]
    work = []
    for group in range(groups):
        turned = pltpu.roll(packed, (columns - group * vectors) % columns, 1)
        unit = jnp.where(lane - vectors == sub + group * SUB, 1.0, 0.0)
        work.append(jnp.where(lane < vectors, turned, unit))
    for home in range(groups):
        first = home * SUB
        column = {
            (group, j): jnp.broadcast_to(work[group][:, first + j : first + j + 1], shape)
            for group in range(home, groups)
            for j in range(SUB)
        }
        for at in range(SUB):
            inverse_pivot = jnp.broadcast_to((1.0 / column[home, at])[at : at + 1, :], shape)
            line = jnp.broadcast_to(work[home][at : at + 1, :], shape)
            for group in range(home, groups):
                factor = column[group, at] * inverse_pivot
                if group == home:
                    factor = jnp.where(sub > at, factor, 0.0)
                for j in range(at + 1, SUB):
                    level = jnp.broadcast_to(column[home, j][at : at + 1, :], shape)
                    if group == home:
                        column[home, j, "next"] = column[home, j] - factor * level
                    else:
                        column[group, j] = column[group, j] - factor * level
                work[group] = work[group] - factor * line
            for j in range(at + 1, SUB):
                column[home, j] = column.pop((home, j, "next"))
    inverse = []
    for group in range(groups):
        row = sub + group * SUB
        pivot = jnp.sum(jnp.where(lane == row, work[group], 0.0), axis=1, keepdims=True)
        done = work[group] * (1.0 / jnp.sqrt(jnp.broadcast_to(pivot, shape)))
        upper[pl.ds(group * SUB, SUB), :] = jnp.where(lane >= row, done, 0.0)[:, :vectors]
        inverse.append(pltpu.roll(done, columns - vectors, 1)[:, :vectors])
    inverse = jnp.concatenate(inverse, axis=0)
    stride = layers * rows
    at_edge = jnp.logical_or(lane < 2, lane >= columns - 2)
    wide = 2 if stride % 2 == 0 else 1

    def whole(at):
        layer, row = divmod(at, rows)
        parts = []
        for group in range(groups):
            edge = sides[pl.ds(layer * vectors + group * SUB, SUB), :]
            edge = pltpu.roll(edge, -(SPAN * (row + 2) + EDGE) % columns, 1)
            here = evolved[pl.ds(group * SUB, SUB), pl.ds(at * columns, columns)]
            parts.append(jnp.where(at_edge, edge, here))
        return jnp.concatenate(parts, axis=0)

    for first in range(0, stride, wide):
        part = jnp.dot(
            inverse, jnp.concatenate([whole(first + n) for n in range(wide)], axis=1),
            precision=lax.Precision.HIGHEST, preferred_element_type=jnp.float32,
        )
        for n in range(wide):
            for group in range(groups):
                at = pl.ds(group * SUB * stride + first + n, SUB, stride=stride)
                basis[at, :] = part[group * SUB : (group + 1) * SUB, n * columns : (n + 1) * columns]


def exchange(value, axis, partner):
    count = lax.axis_size(axis)
    return lax.ppermute(value, axis, [(i, partner(i)) for i in range(count)])


def local(base_stream, tangent_vectors):
    sizes = tangent_vectors.shape
    vectors, layers, rows, columns = sizes
    down, across = lax.axis_size("gy"), lax.axis_size("gx")
    assert layers == 2 and down & (down - 1) == 0 and across & (across - 1) == 0 and across > 1
    assert (rows + 4) * SPAN <= columns and columns >= 2 * SPAN and vectors * vectors == SUB * columns
    pv = tangent_vectors.reshape(vectors * layers * rows, columns)
    base = base_stream.reshape(layers * rows, columns)
    f32 = lambda *shape: jax.ShapeDtypeStruct(shape, jnp.float32)

    def call(body, outs, *operands, scratch=(), inputs=VMEM):
        return pl.pallas_call(
            lambda *refs: body(sizes, *refs),
            out_shape=outs,
            in_specs=[inputs] * len(operands),
            out_specs=[VMEM] * len(outs),
            scratch_shapes=scratch,
            compiler_params=pltpu.CompilerParams(vmem_limit_bytes=8 << 20),
        )(*operands)

    strip = f32(layers * 2 * vectors + SUB, columns)
    bottom, top = call(
        pack_rows_body, [strip, strip],
        pltpu.with_memory_space_constraint(tangent_vectors.reshape(vectors * layers, rows, columns), pltpu.HBM),
        pltpu.with_memory_space_constraint(base, pltpu.HBM),
        inputs=pl.BlockSpec(memory_space=pltpu.HBM),
        scratch=[
            pltpu.VMEM((vectors * layers, rows, columns), jnp.float32),
            pltpu.VMEM((layers * rows, columns), jnp.float32),
            pltpu.SemaphoreType.DMA((3,)),
        ],
    )
    above = exchange(bottom, "gy", lambda i: (i + 1) % down)
    below = exchange(top, "gy", lambda i: (i - 1) % down)
    cells = layers * rows * columns
    scale = 1.0 / (cells * down * across)
    parcel = f32(SUB + layers * (vectors + SUB), columns)
    evolved, message = call(
        lambda sizes, *refs: stencil_body(sizes, scale, *refs),
        [f32(vectors, cells), parcel],
        pv, base, above, below,
        scratch=[pltpu.VMEM((layers * rows, 4, SUB, columns), jnp.float32)],
    )
    half, sides = 1, ()
    while half < across:
        last = 2 * half == across
        got = exchange(message, "gx", lambda i: i ^ (2 * half - 1))
        body = lambda sizes, *refs, half=half, last=last: join_body(sizes, scale, half, last, *refs)
        message, *sides = call(
            body,
            [f32(SUB, columns) if last else parcel, f32(layers * vectors, columns)],
            message, got, *sides,
            scratch=[pltpu.VMEM((vectors, (2 if last else 1) * layers * columns), jnp.float32)],
        )
        half *= 2
    gram = message
    half = 1
    while half < down:
        gram = gram + exchange(gram, ("gy", "gx"), lambda i: ((i // across) ^ half) * across + ((i % across) ^ 1))
        half *= 2
    basis, upper = call(
        basis_body, [f32(vectors * layers * rows, columns), f32(vectors, vectors)], evolved, *sides, gram
    )
    return basis.reshape(sizes), upper


def solution(mesh):
    return jax.shard_map(
        local,
        mesh=mesh,
        in_specs=(P("ens", "gy", "gx"), P("ens", None, "gy", "gx")),
        out_specs=(P("ens", None, "gy", "gx"), P("ens", None)),
        check_vma=False,
    )
```

time: 29.2 us -> 25.8 us (0.88)
  blocking collectives: 11.2 us -> 0 us
  waiting for transfers between devices: 5.54 us -> 11.1 us
  starting transfers between devices: 7.26 us -> 9.02 us
  Pallas kernels: 4.28 us -> 4.9 us
    all_to_all x1 -> x0, blocking collectives: 11.2 us -> none  [local(): gram = lax.all_to_all(spread, ('gy', 'gx'), 0, 0, tiled=True).sum(0)]
    ppermute x4 -> x6, waiting for transfers between devices: 5.54 us -> 11.1 us  [exchange(): return lax.ppermute(value, axis, [(i, partner(i)) for i in range(count)])]
    ppermute x4 -> x6, starting transfers between devices: 7.26 us -> 9.02 us  [exchange(): return lax.ppermute(value, axis, [(i, partner(i)) for i in range(count)])]
    pallas_call x4 -> x5, Pallas kernels: 4.28 us -> 4.9 us  [call(): pl.pallas_call(lambda *refs: body(sizes, *refs), out_shape=outs, in_specs...]
  transfers between devices with their start and end apart: 4 -> 6, of which waited for: 2 -> 6; matrix products, arithmetic and copies ran while one was open for 0% -> 0% of each run, Pallas kernels for 0% -> 0%
where the time goes in v3:
time: 25.8 us; the launch traced here: 25.7 us
  waiting for transfers between devices  11.1 us (43%)
  starting transfers between devices  9.02 us (35%)
  Pallas kernels  4.9 us (19%)
  between operations  0.67 us (3%)
    ppermute x6, waiting for transfers between devices, exchange(): return lax.ppermute(value, axis, [(i, partner(i)) for i in range(count)])  11.1 us
    ppermute x6, starting transfers between devices, exchange(): return lax.ppermute(value, axis, [(i, partner(i)) for i in range(count)])  9.02 us
    pallas_call x5, Pallas kernels, call(): pl.pallas_call(lambda *refs: body(sizes, *refs), out_shape=outs, in_specs...  4.9 us
  transfers between devices with their start and end apart: 6, of which 6 were waited for; matrix products, arithmetic and copies ran while one was open for 0% of the time, Pallas kernels for 0%

profile of v3, /device:TPU:0, one launch (start us, length us, event | category | flops | bytes accessed | tf_op | source)
XLA Modules:
  0.0 25.7 jit_solution(11015770421493217830)
XLA Ops:
  0.6 0.0 copy-start
  0.6 0.0 copy-start.1
  0.6 1.0 %shard_map.41 = (f32[136,128]{1,0:T(8,128)S(1)}, f32[136,128]{1,0:T(8,128)S(1)}) custom-call(f32[64,8,128]{2,1,0:T(8,128)} %bitcast.4, f32[16,128]{1,0:T(8,128)} %bitcast.6), custom_call_target="tpu_custom_call" | custom-call | tf_op jit(solution)/shard_map/pallas_call | solution.py:317
  1.6 3.1 %collective-permute-start = (f32[136,128]{1,0:T(8,128)S(1)}, f32[136,128]{1,0:T(8,128)S(1)}, u32[]{:S(2)}, u32[]{:S(2)}) collective-permute-start(f32[136,128]{1,0:T(8,128)S(1)} %get-tuple-element.12), channel_id=1, source_target_pairs={{0,4},{4,8},{8,12},{12,0},{1,5},{5,9},{9,13},{13,1},{2,6},{6,10},{... | collective-permute-start | bytes 208904 | tf_op jit(solution)/shard_map/ppermute | solution.py:303
  4.7 2.1 %collective-permute-start.1 = (f32[136,128]{1,0:T(8,128)S(1)}, f32[136,128]{1,0:T(8,128)S(1)}, u32[]{:S(2)}, u32[]{:S(2)}) collective-permute-start(f32[136,128]{1,0:T(8,128)S(1)} %get-tuple-element.13), channel_id=1, source_target_pairs={{0,12},{4,0},{8,4},{12,8},{1,13},{5,1},{9,5},{13,9},{2,14},{6,2},{... | collective-permute-start | bytes 208904 | tf_op jit(solution)/shard_map/ppermute | solution.py:303
  6.8 2.4 %collective-permute-done.refs_2_ = f32[136,128]{1,0:T(8,128)S(1)} collective-permute-done((f32[136,128]{1,0:T(8,128)S(1)}, f32[136,128]{1,0:T(8,128)S(1)}, u32[]{:S(2)}, u32[]{:S(2)}) %collective-permute-start) | collective-permute-done | bytes 69664 | tf_op jit(solution)/shard_map/ppermute | solution.py:303
  9.2 0.7 %collective-permute-done.1.refs_3_ = f32[136,128]{1,0:T(8,128)S(1)} collective-permute-done((f32[136,128]{1,0:T(8,128)S(1)}, f32[136,128]{1,0:T(8,128)S(1)}, u32[]{:S(2)}, u32[]{:S(2)}) %collective-permute-start.1) | collective-permute-done | bytes 69664 | tf_op jit(solution)/shard_map/ppermute | solution.py:303
  9.9 0.0 copy-done
  9.9 0.0 copy-done.1
  9.9 0.9 %shard_map.42 = (f32[32,2048]{1,0:T(8,128)S(1)}, f32[88,128]{1,0:T(8,128)S(1)}) custom-call(f32[512,128]{1,0:T(8,128)S(1)} %bitcast.5, f32[16,128]{1,0:T(8,128)S(1)} %bitcast.7, f32[136,128]{1,0:T(8,128)S(1)} %collective-permute-done.refs_2_, f32[136,128]{1,0:T(8,128)S(1)} %collective-permute-done.1.refs_3_), custom_call_target="tpu_custom_call" | custom-call | tf_op jit(solution)/shard_map/pallas_call | solution.py:317
  10.8 0.0 collective-permute-start.2
  10.8 1.2 %collective-permute-done.2.refs_1_ = f32[88,128]{1,0:T(8,128)S(1)} collective-permute-done((f32[88,128]{1,0:T(8,128)S(1)}, f32[88,128]{1,0:T(8,128)S(1)}, u32[]{:S(2)}, u32[]{:S(2)}) %collective-permute-start.2) | collective-permute-done | bytes 45088 | tf_op jit(solution)/shard_map/ppermute | solution.py:303
  12.1 0.4 %shard_map.43 = (f32[88,128]{1,0:T(8,128)S(1)}, f32[64,128]{1,0:T(8,128)S(1)}) custom-call(f32[88,128]{1,0:T(8,128)S(1)} %get-tuple-element.15.refs_0_, f32[88,128]{1,0:T(8,128)S(1)} %collective-permute-done.2.refs_1_), custom_call_target="tpu_custom_call" | custom-call | tf_op jit(solution)/shard_map/pallas_call | solution.py:317
  12.5 1.3 %collective-permute-start.3 = (f32[88,128]{1,0:T(8,128)S(1)}, f32[88,128]{1,0:T(8,128)S(1)}, u32[]{:S(2)}, u32[]{:S(2)}) collective-permute-start(f32[88,128]{1,0:T(8,128)S(1)} %get-tuple-element.16.refs_0_), channel_id=1, source_target_pairs={{0,3},{1,2},{2,1},{3,0},{4,7},{5,6},{6,5},{7,4},{8,11},{9,10},{10,... | collective-permute-start | bytes 135176 | tf_op jit(solution)/shard_map/ppermute | solution.py:303
  13.8 2.4 %collective-permute-done.3.refs_1_ = f32[88,128]{1,0:T(8,128)S(1)} collective-permute-done((f32[88,128]{1,0:T(8,128)S(1)}, f32[88,128]{1,0:T(8,128)S(1)}, u32[]{:S(2)}, u32[]{:S(2)}) %collective-permute-start.3) | collective-permute-done | bytes 45088 | tf_op jit(solution)/shard_map/ppermute | solution.py:303
  16.1 0.6 %shard_map.44 = (f32[8,128]{1,0:T(8,128)S(1)}, f32[64,128]{1,0:T(8,128)S(1)}) custom-call(f32[88,128]{1,0:T(8,128)S(1)} %get-tuple-element.16.refs_0_, f32[88,128]{1,0:T(8,128)S(1)} %collective-permute-done.3.refs_1_, f32[64,128]{1,0:T(8,128)S(1)} %get-tuple-element.17.refs_2_), custom_call_target="tpu_custom_call" | custom-call | tf_op jit(solution)/shard_map/pallas_call | solution.py:317
  16.7 0.9 %collective-permute-start.4 = (f32[8,128]{1,0:T(8,128)S(1)}, f32[8,128]{1,0:T(8,128)S(1)}, u32[]{:S(2)}, u32[]{:S(2)}) collective-permute-start(f32[8,128]{1,0:T(8,128)S(1)} %get-tuple-element.19), channel_id=1, source_target_pairs={{0,5},{1,4},{2,7},{3,6},{4,1},{5,0},{6,3},{7,2},{8,13},{9,12},{10,... | collective-permute-start | bytes 12296 | tf_op jit(solution)/shard_map/ppermute | solution.py:303
  17.6 2.1 %collective-permute-done.4 = f32[8,128]{1,0:T(8,128)S(1)} collective-permute-done((f32[8,128]{1,0:T(8,128)S(1)}, f32[8,128]{1,0:T(8,128)S(1)}, u32[]{:S(2)}, u32[]{:S(2)}) %collective-permute-start.4) | collective-permute-done | bytes 4128 | tf_op jit(solution)/shard_map/ppermute | solution.py:303
  19.8 1.6 %collective-permute-start.5 = (f32[8,128]{1,0:T(8,128)S(1)}, f32[8,128]{1,0:T(8,128)S(1)}, u32[]{:S(2)}, u32[]{:S(2)}) collective-permute-start(f32[8,128]{1,0:T(8,128)S(1)} %add.6), channel_id=1, source_target_pairs={{0,9},{1,8},{2,11},{3,10},{4,13},{5,12},{6,15},{7,14},{8,1},{9,0},... | collective-permute-start | bytes 12296 | tf_op jit(solution)/shard_map/ppermute | solution.py:303
  21.4 2.3 %collective-permute-done.5 = f32[8,128]{1,0:T(8,128)S(1)} collective-permute-done((f32[8,128]{1,0:T(8,128)S(1)}, f32[8,128]{1,0:T(8,128)S(1)}, u32[]{:S(2)}, u32[]{:S(2)}) %collective-permute-start.5) | collective-permute-done | bytes 4128 | tf_op jit(solution)/shard_map/ppermute | solution.py:303
  23.7 2.0 %shard_map.45 = (f32[512,128]{1,0:T(8,128)}, f32[32,32]{1,0:T(8,128)}) custom-call(f32[32,2048]{1,0:T(8,128)S(1)} %get-tuple-element.14.refs_0_, f32[64,128]{1,0:T(8,128)S(1)} %get-tuple-element.18.refs_1_, f32[8,128]{1,0:T(8,128)S(1)} %add.7.refs_2_), custom_call_target="tpu_custom_call" | custom-call | tf_op jit(solution)/shard_map/pallas_call | solution.py:317
  (2 shorter events, 0.0 us)
Async XLA Ops:
  0.6 9.3 %copy-start = (f32[32,2,8,128]{3,2,1,0:T(8,128)S(1)}, f32[32,2,8,128]{3,2,1,0:T(8,128)}, u32[]{:S(2)}) copy-start(f32[32,2,8,128]{3,2,1,0:T(8,128)} %param.3) | copy-start | bytes 786436
  0.6 9.2 %copy-start.1 = (f32[2,8,128]{2,1,0:T(8,128)S(1)}, f32[2,8,128]{2,1,0:T(8,128)}, u32[]{:S(2)}) copy-start(f32[2,8,128]{2,1,0:T(8,128)} %param.2) | copy-start | bytes 24580
  1.6 7.6 %collective-permute-start = (f32[136,128]{1,0:T(8,128)S(1)}, f32[136,128]{1,0:T(8,128)S(1)}, u32[]{:S(2)}, u32[]{:S(2)}) collective-permute-start(f32[136,128]{1,0:T(8,128)S(1)} %get-tuple-element.12), channel_id=1, source_target_pairs={{0,4},{4,8},{8,12},{12,0},{1,5},{5,9},{9,13},{13,1},{2,6},{6,10},{... | collective-permute-start | bytes 208904 | tf_op jit(solution)/shard_map/ppermute | solution.py:303
  4.7 5.1 %collective-permute-start.1 = (f32[136,128]{1,0:T(8,128)S(1)}, f32[136,128]{1,0:T(8,128)S(1)}, u32[]{:S(2)}, u32[]{:S(2)}) collective-permute-start(f32[136,128]{1,0:T(8,128)S(1)} %get-tuple-element.13), channel_id=1, source_target_pairs={{0,12},{4,0},{8,4},{12,8},{1,13},{5,1},{9,5},{13,9},{2,14},{6,2},{... | collective-permute-start | bytes 208904 | tf_op jit(solution)/shard_map/ppermute | solution.py:303
  10.8 1.2 %collective-permute-start.2 = (f32[88,128]{1,0:T(8,128)S(1)}, f32[88,128]{1,0:T(8,128)S(1)}, u32[]{:S(2)}, u32[]{:S(2)}) collective-permute-start(f32[88,128]{1,0:T(8,128)S(1)} %get-tuple-element.15.refs_0_), channel_id=1, source_target_pairs={{0,1},{1,0},{2,3},{3,2},{4,5},{5,4},{6,7},{7,6},{8,9},{9,8},{10,11... | collective-permute-start | bytes 135176 | tf_op jit(solution)/shard_map/ppermute | solution.py:303
  12.5 3.6 %collective-permute-start.3 = (f32[88,128]{1,0:T(8,128)S(1)}, f32[88,128]{1,0:T(8,128)S(1)}, u32[]{:S(2)}, u32[]{:S(2)}) collective-permute-start(f32[88,128]{1,0:T(8,128)S(1)} %get-tuple-element.16.refs_0_), channel_id=1, source_target_pairs={{0,3},{1,2},{2,1},{3,0},{4,7},{5,6},{6,5},{7,4},{8,11},{9,10},{10,... | collective-permute-start | bytes 135176 | tf_op jit(solution)/shard_map/ppermute | solution.py:303
  16.7 3.1 %collective-permute-start.4 = (f32[8,128]{1,0:T(8,128)S(1)}, f32[8,128]{1,0:T(8,128)S(1)}, u32[]{:S(2)}, u32[]{:S(2)}) collective-permute-start(f32[8,128]{1,0:T(8,128)S(1)} %get-tuple-element.19), channel_id=1, source_target_pairs={{0,5},{1,4},{2,7},{3,6},{4,1},{5,0},{6,3},{7,2},{8,13},{9,12},{10,... | collective-permute-start | bytes 12296 | tf_op jit(solution)/shard_map/ppermute | solution.py:303
  19.8 3.9 %collective-permute-start.5 = (f32[8,128]{1,0:T(8,128)S(1)}, f32[8,128]{1,0:T(8,128)S(1)}, u32[]{:S(2)}, u32[]{:S(2)}) collective-permute-start(f32[8,128]{1,0:T(8,128)S(1)} %add.6), channel_id=1, source_target_pairs={{0,9},{1,8},{2,11},{3,10},{4,13},{5,12},{6,15},{7,14},{8,1},{9,0},... | collective-permute-start | bytes 12296 | tf_op jit(solution)/shard_map/ppermute | solution.py:303

commit v4 on v3

--- a/solution.py
+++ b/solution.py
@@ -97,66 +97,124 @@
     return result + weights[3] * (at.near_dy + cross * other.dy)
 
 
-def packed_gram(whole, scale):
-    local = lax.dot_general(
+def gram_of(whole, scale):
+    return lax.dot_general(
         whole, whole, (((1,), (1,)), ((), ())),
         precision=lax.Precision.HIGHEST, preferred_element_type=jnp.float32,
     ) * scale
-    return jnp.concatenate([local[at : at + SUB] for at in range(0, whole.shape[0], SUB)], axis=1)
-
-
-def stencil_body(sizes, scale, pv, base, above, below, evolved, message, coef):
-    vectors, layers, rows, columns = sizes
-    source = Rows(sizes, pv, base, above, below)
-    lane = lanes_of((SUB, columns))
-    inside = jnp.logical_and(lane >= 2, lane < columns - 2)
-    place = lane // SPAN
-
-    def fields(group):
-        value, dx, sx, dx2, sx2 = {}, {}, {}, {}, {}
-        for layer in range(layers):
-            edges = jnp.zeros((SUB, columns), jnp.float32)
-            for row in range(-2, rows + 2):
-                here = source.get(layer, row, group)
-                value[layer, row] = here
+
+
+def at_end(part, columns):
+    return jnp.concatenate([jnp.zeros((SUB, columns - part.shape[1]), jnp.float32), part], axis=1)
+
+
+def tile_fields(source, group, wanted, edge_rows, edges):
+    layers, columns = source.layers, source.columns
+    place = lanes_of((SUB, columns)) // SPAN
+    value, dx, sx, dx2, sx2 = {}, {}, {}, {}, {}
+    spread = sorted({row + n for row in wanted for n in range(-2, 3)} | set(edge_rows))
+    beside = {row + n for row in wanted for n in range(-1, 2)}
+    for layer in range(layers):
+        packed = edges(layer, None)
+        for row in spread:
+            here = source.get(layer, row, group)
+            value[layer, row] = here
+            if row in edge_rows:
                 turned = pltpu.roll(here, (EDGE + SPAN * (row + 2)) % columns, 1)
-                edges = jnp.where(place == row + 2, turned, edges)
-                if row == -2 or row == rows + 1:
-                    continue
+                packed = jnp.where(place == row + 2, turned, packed)
+            if row in beside:
                 west, east = pltpu.roll(here, 1, 1), pltpu.roll(here, columns - 1, 1)
                 dx[layer, row], sx[layer, row] = east - west, east + west
-                if 0 <= row < rows:
-                    west, east = pltpu.roll(here, 2, 1), pltpu.roll(here, columns - 2, 1)
-                    dx2[layer, row], sx2[layer, row] = east - west, east + west
-            message[pl.ds(SUB + layer * (vectors + SUB) + group * SUB, SUB), :] = edges
-        found = {}
-        for layer in range(layers):
-            for row in range(rows):
-                up, down = (layer, row - 1), (layer, row + 1)
-                at = found[layer, row] = Fields()
-                at.value, at.dx = value[layer, row], dx[layer, row]
-                at.dy = value[down] - value[up]
-                at.near = sx[layer, row] + (value[down] + value[up])
-                at.near_dx = dx2[layer, row] + (dx[down] + dx[up])
-                at.near_dy = (sx[down] - sx[up]) + (value[layer, row + 2] - value[layer, row - 2])
-                at.diagonal = sx[down] + sx[up]
-                at.far = sx2[layer, row] + (value[layer, row + 2] + value[layer, row - 2])
-        return found
-
-    found = fields(source.groups)
+            if row in wanted:
+                west, east = pltpu.roll(here, 2, 1), pltpu.roll(here, columns - 2, 1)
+                dx2[layer, row], sx2[layer, row] = east - west, east + west
+        edges(layer, packed)
+    found = {}
     for layer in range(layers):
-        for row in range(rows):
-            for n, weight in enumerate(base_weights(found[layer, row], found[1 - layer, row], layer)):
-                coef[layer * rows + row, n] = weight
-    for group in range(source.groups):
-        found = fields(group)
-        for layer in range(layers):
-            for row in range(rows):
-                at = layer * rows + row
-                weights = [coef[at, n] for n in range(4)]
-                result = stepped(found[layer, row], found[1 - layer, row], layer, weights)
-                evolved[pl.ds(group * SUB, SUB), pl.ds(at * columns, columns)] = jnp.where(inside, result, 0.0)
-    message[pl.ds(0, SUB), :] = packed_gram(evolved[...], scale)
+        for row in wanted:
+            up, down = (layer, row - 1), (layer, row + 1)
+            at = found[layer, row] = Fields()
+            at.value, at.dx = value[layer, row], dx[layer, row]
+            at.dy = value[down] - value[up]
+            at.near = sx[layer, row] + (value[down] + value[up])
+            at.near_dx = dx2[layer, row] + (dx[down] + dx[up])
+            at.near_dy = (sx[down] - sx[up]) + (value[layer, row + 2] - value[layer, row - 2])
+            at.diagonal = sx[down] + sx[up]
+            at.far = sx2[layer, row] + (value[layer, row + 2] + value[layer, row - 2])
+    return found
+
+
+def step_rows(source, wanted, edge_rows, edges_of, evolved, coef):
+    lane = lanes_of((SUB, source.columns))
+    inside = jnp.logical_and(lane >= 2, lane < source.columns - 2)
+    order = [source.groups, *range(source.groups)]
+    for group in order:
+        found = tile_fields(source, group, wanted, edge_rows, edges_of(group))
+        for layer in range(source.layers):
+            for n, row in enumerate(wanted):
+                at = layer * len(wanted) + n
+                here, other = found[layer, row], found[1 - layer, row]
+                if group == source.groups:
+                    for w, weight in enumerate(base_weights(here, other, layer)):
+                        coef[at, w] = weight
+                    continue
+                result = stepped(here, other, layer, [coef[at, w] for w in range(4)])
+                block = pl.ds(group * SUB, SUB), pl.ds(at * source.columns, source.columns)
+                evolved[block] = jnp.where(inside, result, 0.0)
+
+
+def edge_place(sizes, layer, group):
+    vectors, layers = sizes[:2]
+    if group < vectors // SUB:
+        return pl.ds(layer * vectors + group * SUB, SUB)
+    return pl.ds(layers * vectors + layer, 1)
+
+
+def row_sets(rows):
+    return tuple(range(2, rows - 2)), (0, 1, rows - 2, rows - 1)
+
+
+def middle_body(sizes, scale, pv, base, evolved, gram, edges, coef):
+    vectors, layers, rows, columns = sizes
+    source = Rows(sizes, pv, base, None, None)
+
+    def edges_of(group):
+        def put(layer, packed):
+            if packed is None:
+                return jnp.zeros((SUB, columns), jnp.float32)
+            at = edge_place(sizes, layer, group)
+            edges[at, :] = packed[: at.size]
+
+        return put
+
+    wanted, _ = row_sets(rows)
+    step_rows(source, wanted, range(rows), edges_of, evolved, coef)
+    edges[pl.ds(layers * (vectors + 1), SUB - layers), :] = jnp.zeros((SUB - layers, columns), jnp.float32)
+    local = gram_of(evolved[...], scale)
+    for at in range(0, vectors, SUB):
+        gram[pl.ds(at, SUB), :] = at_end(local[at : at + SUB], columns)
+
+
+def border_body(sizes, scale, pv, base, above, below, gram, edges, evolved, message, coef):
+    vectors, layers, rows, columns = sizes
+    source = Rows(sizes, pv, base, above, below)
+    halo = (-2, -1, rows, rows + 1)
+
+    def edges_of(group):
+        def put(layer, packed):
+            at = edge_place(sizes, layer, group)
+            if packed is None:
+                return jnp.broadcast_to(edges[at, :], (SUB, columns))
+            message[at, :] = packed[: at.size]
+
+        return put
+
+    _, wanted = row_sets(rows)
+    step_rows(source, wanted, halo, edges_of, evolved, coef)
+    message[pl.ds(layers * (vectors + 1), SUB - layers), :] = jnp.zeros((SUB - layers, columns), jnp.float32)
+    local = gram_of(evolved[...], scale)
+    for at in range(0, vectors, SUB):
+        message[pl.ds(at, SUB), :] = message[pl.ds(at, SUB), :] + (gram[pl.ds(at, SUB), :] + at_end(local[at : at + SUB], columns))
 
 
 def strip_fields(here, columns):
@@ -200,14 +258,18 @@
     keep_wrap = jnp.logical_or(jnp.logical_and(west_half, spot == 2 * half - 1), jnp.logical_and(~west_half, spot == 0))
     kinds = (False, True) if last else (False,)
     weights = {}
+    parcel = {}
     for group in (groups, *range(groups)):
         found = {}
         for layer in range(layers):
-            at = pl.ds(SUB + layer * (vectors + SUB) + group * SUB, SUB)
+            at = edge_place(sizes, layer, group)
             here, there = mine[at, :], got[at, :]
+            if group < groups and layer == 0:
+                parcel[group] = here + there
+            here, there = jnp.broadcast_to(here, shape), jnp.broadcast_to(there, shape)
             mid, outer = jnp.where(mid_mine, here, there), jnp.where(mid_mine, there, here)
             if not last:
-                message[at, :] = outer
+                message[at, :] = outer[: at.size]
             found[layer, False] = strip_fields(mid, columns)
             if last:
                 found[layer, True] = strip_fields(outer, columns)
@@ -226,11 +288,46 @@
                 own = jnp.where(keep_wrap if wrap else keep_mid, result, own)
                 if wrap == last:
                     sides[where, :] = own
-    head = pl.ds(0, SUB)
-    message[head, :] = (mine[head, :] + got[head, :]) + packed_gram(strips[...], scale)
-
-
-def basis_body(sizes, evolved, sides, gram, basis, upper):
+    if not last:
+        message[pl.ds(layers * (vectors + 1), SUB - layers), :] = jnp.zeros((SUB - layers, columns), jnp.float32)
+    local = gram_of(strips[...], scale)
+    total = jnp.zeros(shape, jnp.float32)
+    free = columns - vectors
+    for group in range(groups):
+        block = pl.ds(group * SUB, SUB)
+        joined = parcel[group] + at_end(local[group * SUB : (group + 1) * SUB], columns)
+        if last:
+            turned = pltpu.roll(joined, (vectors * (group + 1)) % columns, 1) if group + 1 < groups else joined
+            total = jnp.where(lane // vectors == group, turned, total)
+        else:
+            message[block, :] = jnp.where(lane >= free, joined, message[block, :])
+    if last:
+        message[...] = total
+
+
+def ready_body(sizes, middle, border, sides, parts):
+    vectors, layers, rows, columns = sizes
+    lane = lanes_of((SUB * 2, columns))
+    at_edge = jnp.logical_or(lane < 2, lane >= columns - 2)
+    sets = row_sets(rows)
+    pair = 2 * SUB
+    for layer in range(layers):
+        for row in range(rows):
+            which = 0 if row in sets[0] else 1
+            block = layer * len(sets[which]) + sets[which].index(row)
+            for first in range(0, vectors, pair):
+                edge = sides[pl.ds(layer * vectors + first, pair), :]
+                edge = pltpu.roll(edge, -(SPAN * (row + 2) + EDGE) % columns, 1)
+                here = (middle, border)[which][pl.ds(first, pair), pl.ds(block * columns, columns)]
+                rest = jnp.where(at_edge, edge, here)
+                for n in range(3):
+                    part = rest.astype(jnp.bfloat16)
+                    if n < 2:
+                        rest = rest - part.astype(jnp.float32)
+                    parts[pl.ds(n * vectors + first, pair), pl.ds((layer * rows + row) * columns, columns)] = part
+
+
+def basis_body(sizes, parts, gram, basis, upper):
     vectors, layers, rows, columns = sizes
     groups = vectors // SUB
     shape = (SUB, columns)
@@ -265,32 +362,35 @@
                 work[group] = work[group] - factor * line
             for j in range(at + 1, SUB):
                 column[home, j] = column.pop((home, j, "next"))
+    order = ((0, 0), (1, 0), (2, 0), (0, 1), (1, 1), (0, 2))
+    slot = lane // vectors
     inverse = []
     for group in range(groups):
         row = sub + group * SUB
         pivot = jnp.sum(jnp.where(lane == row, work[group], 0.0), axis=1, keepdims=True)
         done = work[group] * (1.0 / jnp.sqrt(jnp.broadcast_to(pivot, shape)))
         upper[pl.ds(group * SUB, SUB), :] = jnp.where(lane >= row, done, 0.0)[:, :vectors]
-        inverse.append(pltpu.roll(done, columns - vectors, 1)[:, :vectors])
-    inverse = jnp.concatenate(inverse, axis=0)
+        rest, terms = jnp.where(slot == 1, done, 0.0), []
+        for _ in range(3):
+            term = rest.astype(jnp.bfloat16).astype(jnp.float32)
+            rest = rest - term
+            terms.append(term)
+        per = columns // vectors
+        wide = []
+        for first in range(0, len(order), per):
+            line = jnp.zeros(shape, jnp.float32)
+            for n, (mine, _) in enumerate(order[first : first + per]):
+                line = line + pltpu.roll(terms[mine], (n - 1) * vectors % columns, 1)
+            wide.append(line)
+        inverse.append(jnp.concatenate(wide, axis=1))
+    inverse = jnp.concatenate(inverse, axis=0).astype(jnp.bfloat16)[:, : len(order) * vectors]
     stride = layers * rows
-    at_edge = jnp.logical_or(lane < 2, lane >= columns - 2)
     wide = 2 if stride % 2 == 0 else 1
-
-    def whole(at):
-        layer, row = divmod(at, rows)
-        parts = []
-        for group in range(groups):
-            edge = sides[pl.ds(layer * vectors + group * SUB, SUB), :]
-            edge = pltpu.roll(edge, -(SPAN * (row + 2) + EDGE) % columns, 1)
-            here = evolved[pl.ds(group * SUB, SUB), pl.ds(at * columns, columns)]
-            parts.append(jnp.where(at_edge, edge, here))
-        return jnp.concatenate(parts, axis=0)
-
     for first in range(0, stride, wide):
+        at = pl.ds(first * columns, wide * columns)
+        split = [parts[pl.ds(n * vectors, vectors), at] for n in range(3)]
         part = jnp.dot(
-            inverse, jnp.concatenate([whole(first + n) for n in range(wide)], axis=1),
-            precision=lax.Precision.HIGHEST, preferred_element_type=jnp.float32,
+            inverse, jnp.concatenate([split[n] for _, n in order], axis=0), preferred_element_type=jnp.float32
         )
         for n in range(wide):
             for group in range(groups):
@@ -308,7 +408,8 @@
     vectors, layers, rows, columns = sizes
     down, across = lax.axis_size("gy"), lax.axis_size("gx")
     assert layers == 2 and down & (down - 1) == 0 and across & (across - 1) == 0 and across > 1
-    assert (rows + 4) * SPAN <= columns and columns >= 2 * SPAN and vectors * vectors == SUB * columns
+    assert rows >= 5 and (rows + 4) * SPAN + vectors <= columns and vectors * vectors == SUB * columns
+    assert vectors % (2 * SUB) == 0
     pv = tangent_vectors.reshape(vectors * layers * rows, columns)
     base = base_stream.reshape(layers * rows, columns)
     f32 = lambda *shape: jax.ShapeDtypeStruct(shape, jnp.float32)
@@ -339,12 +440,19 @@
     below = exchange(top, "gy", lambda i: (i - 1) % down)
     cells = layers * rows * columns
     scale = 1.0 / (cells * down * across)
-    parcel = f32(SUB + layers * (vectors + SUB), columns)
-    evolved, message = call(
-        lambda sizes, *refs: stencil_body(sizes, scale, *refs),
-        [f32(vectors, cells), parcel],
-        pv, base, above, below,
-        scratch=[pltpu.VMEM((layers * rows, 4, SUB, columns), jnp.float32)],
+    parcel = f32(layers * vectors + SUB, columns)
+    middle_rows, border_rows = (layers * len(part) for part in row_sets(rows))
+    middle, gram, edges = call(
+        lambda sizes, *refs: middle_body(sizes, scale, *refs),
+        [f32(vectors, middle_rows * columns), f32(vectors, columns), parcel],
+        pv, base,
+        scratch=[pltpu.VMEM((middle_rows, 4, SUB, columns), jnp.float32)],
+    )
+    border, message = call(
+        lambda sizes, *refs: border_body(sizes, scale, *refs),
+        [f32(vectors, border_rows * columns), parcel],
+        pv, base, above, below, gram, edges,
+        scratch=[pltpu.VMEM((border_rows, 4, SUB, columns), jnp.float32)],
     )
     half, sides = 1, ()
     while half < across:
@@ -358,13 +466,15 @@
             scratch=[pltpu.VMEM((vectors, (2 if last else 1) * layers * columns), jnp.float32)],
         )
         half *= 2
+    (parts,) = call(ready_body, [jax.ShapeDtypeStruct((3 * vectors, cells), jnp.bfloat16)], middle, border, *sides)
     gram = message
     half = 1
     while half < down:
-        gram = gram + exchange(gram, ("gy", "gx"), lambda i: ((i // across) ^ half) * across + ((i % across) ^ 1))
+        got = exchange(gram, ("gy", "gx"), lambda i: ((i // across) ^ half) * across + ((i % across) ^ 1))
+        gram = gram + got
         half *= 2
     basis, upper = call(
-        basis_body, [f32(vectors * layers * rows, columns), f32(vectors, vectors)], evolved, *sides, gram
+        basis_body, [f32(vectors * layers * rows, columns), f32(vectors, vectors)], parts, gram
     )
     return basis.reshape(sizes), upper
 

time: 25.8 us -> 25.3 us (0.981)
  waiting for transfers between devices: 11.1 us -> 10.1 us
  Pallas kernels: 4.9 us -> 5.28 us
    ppermute x6, waiting for transfers between devices: 11.1 us -> 10.1 us  [exchange(): return lax.ppermute(value, axis, [(i, partner(i)) for i in range(count)])]
    pallas_call x5 -> x7, Pallas kernels: 4.9 us -> 5.28 us  [call(): pl.pallas_call(lambda *refs: body(sizes, *refs), out_shape=outs, in_specs...]
  transfers between devices with their start and end apart: 6 -> 6, of which waited for: 6 -> 6; matrix products, arithmetic and copies ran while one was open for 0% -> 0% of each run, Pallas kernels for 0% -> 3%
where the time goes in v4:
time: 25.3 us; the launch traced here: 25.1 us
  waiting for transfers between devices  10.1 us (40%)
  starting transfers between devices  9.04 us (36%)
  Pallas kernels  5.28 us (21%)
  between operations  0.68 us (3%)
    ppermute x6, waiting for transfers between devices, exchange(): return lax.ppermute(value, axis, [(i, partner(i)) for i in range(count)])  10.1 us
    ppermute x6, starting transfers between devices, exchange(): return lax.ppermute(value, axis, [(i, partner(i)) for i in range(count)])  9.04 us
    pallas_call x7, Pallas kernels, call(): pl.pallas_call(lambda *refs: body(sizes, *refs), out_shape=outs, in_specs...  5.28 us
  transfers between devices with their start and end apart: 6, of which 6 were waited for; matrix products, arithmetic and copies ran while one was open for 0% of the time, Pallas kernels for 3%

profile of v4, /device:TPU:0, one launch (start us, length us, event | category | flops | bytes accessed | tf_op | source)
XLA Modules:
  0.0 25.1 jit_solution(5725605850974375187)
XLA Ops:
  0.6 0.0 copy-start
  0.6 0.0 copy-start.1
  0.6 1.0 %shard_map.42 = (f32[136,128]{1,0:T(8,128)S(1)}, f32[136,128]{1,0:T(8,128)S(1)}) custom-call(f32[64,8,128]{2,1,0:T(8,128)} %bitcast.4, f32[16,128]{1,0:T(8,128)} %bitcast.7), custom_call_target="tpu_custom_call" | custom-call | tf_op jit(solution)/shard_map/pallas_call | solution.py:418
  1.6 3.1 %collective-permute-start = (f32[136,128]{1,0:T(8,128)S(1)}, f32[136,128]{1,0:T(8,128)S(1)}, u32[]{:S(2)}, u32[]{:S(2)}) collective-permute-start(f32[136,128]{1,0:T(8,128)S(1)} %get-tuple-element.16), channel_id=1, source_target_pairs={{0,4},{4,8},{8,12},{12,0},{1,5},{5,9},{9,13},{13,1},{2,6},{6,10},{... | collective-permute-start | bytes 208904 | tf_op jit(solution)/shard_map/ppermute | solution.py:403
  4.7 2.1 %collective-permute-start.1 = (f32[136,128]{1,0:T(8,128)S(1)}, f32[136,128]{1,0:T(8,128)S(1)}, u32[]{:S(2)}, u32[]{:S(2)}) collective-permute-start(f32[136,128]{1,0:T(8,128)S(1)} %get-tuple-element.17), channel_id=1, source_target_pairs={{0,12},{4,0},{8,4},{12,8},{1,13},{5,1},{9,5},{13,9},{2,14},{6,2},{... | collective-permute-start | bytes 208904 | tf_op jit(solution)/shard_map/ppermute | solution.py:403
  6.8 0.0 copy-done
  6.8 0.0 copy-done.1
  6.8 0.6 %shard_map.41 = (f32[32,1024]{1,0:T(8,128)S(1)}, f32[32,128]{1,0:T(8,128)S(1)}, f32[72,128]{1,0:T(8,128)S(1)}) custom-call(f32[512,128]{1,0:T(8,128)S(1)} %bitcast.5, f32[16,128]{1,0:T(8,128)S(1)} %bitcast.8), custom_call_target="tpu_custom_call" | custom-call | tf_op jit(solution)/shard_map/pallas_call | solution.py:418
  7.4 1.8 %collective-permute-done.refs_2_ = f32[136,128]{1,0:T(8,128)S(1)} collective-permute-done((f32[136,128]{1,0:T(8,128)S(1)}, f32[136,128]{1,0:T(8,128)S(1)}, u32[]{:S(2)}, u32[]{:S(2)}) %collective-permute-start) | collective-permute-done | bytes 69664 | tf_op jit(solution)/shard_map/ppermute | solution.py:403
  9.2 0.7 %collective-permute-done.1.refs_3_ = f32[136,128]{1,0:T(8,128)S(1)} collective-permute-done((f32[136,128]{1,0:T(8,128)S(1)}, f32[136,128]{1,0:T(8,128)S(1)}, u32[]{:S(2)}, u32[]{:S(2)}) %collective-permute-start.1) | collective-permute-done | bytes 69664 | tf_op jit(solution)/shard_map/ppermute | solution.py:403
  9.9 0.6 %shard_map.43 = (f32[32,1024]{1,0:T(8,128)S(1)}, f32[72,128]{1,0:T(8,128)S(1)}) custom-call(f32[512,128]{1,0:T(8,128)S(1)} %bitcast.6, f32[16,128]{1,0:T(8,128)S(1)} %bitcast.9, f32[136,128]{1,0:T(8,128)S(1)} %collective-permute-done.refs_2_, f32[136,128]{1,0:T(8,128)S(1)} %collective-permute-done.1.refs_3_, f32[32,128]{1,0:T(8,128)S(1)} %get-tuple-element.18.refs_4_, ...), custom_call_target="tpu_custom_call" | custom-call | tf_op jit(solution)/shard_map/pallas_call | solution.py:418
  10.5 0.0 collective-permute-start.2
  10.6 1.2 %collective-permute-done.2.refs_1_ = f32[72,128]{1,0:T(8,128)S(1)} collective-permute-done((f32[72,128]{1,0:T(8,128)S(1)}, f32[72,128]{1,0:T(8,128)S(1)}, u32[]{:S(2)}, u32[]{:S(2)}) %collective-permute-start.2) | collective-permute-done | bytes 36896 | tf_op jit(solution)/shard_map/ppermute | solution.py:403
  11.8 0.4 %shard_map.44 = (f32[72,128]{1,0:T(8,128)S(1)}, f32[64,128]{1,0:T(8,128)S(1)}) custom-call(f32[72,128]{1,0:T(8,128)S(1)} %get-tuple-element.21.refs_0_, f32[72,128]{1,0:T(8,128)S(1)} %collective-permute-done.2.refs_1_), custom_call_target="tpu_custom_call" | custom-call | tf_op jit(solution)/shard_map/pallas_call | solution.py:418
  12.2 1.3 %collective-permute-start.3 = (f32[72,128]{1,0:T(8,128)S(1)}, f32[72,128]{1,0:T(8,128)S(1)}, u32[]{:S(2)}, u32[]{:S(2)}) collective-permute-start(f32[72,128]{1,0:T(8,128)S(1)} %get-tuple-element.22.refs_0_), channel_id=1, source_target_pairs={{0,3},{1,2},{2,1},{3,0},{4,7},{5,6},{6,5},{7,4},{8,11},{9,10},{10,... | collective-permute-start | bytes 110600 | tf_op jit(solution)/shard_map/ppermute | solution.py:403
  13.5 2.2 %collective-permute-done.3.refs_1_ = f32[72,128]{1,0:T(8,128)S(1)} collective-permute-done((f32[72,128]{1,0:T(8,128)S(1)}, f32[72,128]{1,0:T(8,128)S(1)}, u32[]{:S(2)}, u32[]{:S(2)}) %collective-permute-start.3) | collective-permute-done | bytes 36896 | tf_op jit(solution)/shard_map/ppermute | solution.py:403
  15.6 0.7 %shard_map.45 = (f32[8,128]{1,0:T(8,128)S(1)}, f32[64,128]{1,0:T(8,128)S(1)}) custom-call(f32[72,128]{1,0:T(8,128)S(1)} %get-tuple-element.22.refs_0_, f32[72,128]{1,0:T(8,128)S(1)} %collective-permute-done.3.refs_1_, f32[64,128]{1,0:T(8,128)S(1)} %get-tuple-element.23.refs_2_), custom_call_target="tpu_custom_call" | custom-call | tf_op jit(solution)/shard_map/pallas_call | solution.py:418
  16.3 0.9 %collective-permute-start.4 = (f32[8,128]{1,0:T(8,128)S(1)}, f32[8,128]{1,0:T(8,128)S(1)}, u32[]{:S(2)}, u32[]{:S(2)}) collective-permute-start(f32[8,128]{1,0:T(8,128)S(1)} %get-tuple-element.25), channel_id=1, source_target_pairs={{0,5},{1,4},{2,7},{3,6},{4,1},{5,0},{6,3},{7,2},{8,13},{9,12},{10,... | collective-permute-start | bytes 12296 | tf_op jit(solution)/shard_map/ppermute | solution.py:403
  17.2 2.1 %collective-permute-done.4 = f32[8,128]{1,0:T(8,128)S(1)} collective-permute-done((f32[8,128]{1,0:T(8,128)S(1)}, f32[8,128]{1,0:T(8,128)S(1)}, u32[]{:S(2)}, u32[]{:S(2)}) %collective-permute-start.4) | collective-permute-done | bytes 4128 | tf_op jit(solution)/shard_map/ppermute | solution.py:403
  19.4 1.6 %collective-permute-start.5 = (f32[8,128]{1,0:T(8,128)S(1)}, f32[8,128]{1,0:T(8,128)S(1)}, u32[]{:S(2)}, u32[]{:S(2)}) collective-permute-start(f32[8,128]{1,0:T(8,128)S(1)} %add.6), channel_id=1, source_target_pairs={{0,9},{1,8},{2,11},{3,10},{4,13},{5,12},{6,15},{7,14},{8,1},{9,0},... | collective-permute-start | bytes 12296 | tf_op jit(solution)/shard_map/ppermute | solution.py:403
  21.0 0.2 shard_map.46.refs_0_
  21.1 2.2 %collective-permute-done.5 = f32[8,128]{1,0:T(8,128)S(1)} collective-permute-done((f32[8,128]{1,0:T(8,128)S(1)}, f32[8,128]{1,0:T(8,128)S(1)}, u32[]{:S(2)}, u32[]{:S(2)}) %collective-permute-start.5) | collective-permute-done | bytes 4128 | tf_op jit(solution)/shard_map/ppermute | solution.py:403
  23.3 1.8 %shard_map.47 = (f32[512,128]{1,0:T(8,128)}, f32[32,32]{1,0:T(8,128)}) custom-call(bf16[96,2048]{1,0:T(8,128)(2,1)S(1)} %shard_map.46.refs_0_, f32[8,128]{1,0:T(8,128)S(1)} %add.7.refs_1_), custom_call_target="tpu_custom_call" | custom-call | tf_op jit(solution)/shard_map/pallas_call | solution.py:418
  (2 shorter events, 0.0 us)
Async XLA Ops:
  0.6 6.2 %copy-start = (f32[32,2,8,128]{3,2,1,0:T(8,128)S(1)}, f32[32,2,8,128]{3,2,1,0:T(8,128)}, u32[]{:S(2)}) copy-start(f32[32,2,8,128]{3,2,1,0:T(8,128)} %param.3) | copy-start | bytes 786436
  0.6 6.2 %copy-start.1 = (f32[2,8,128]{2,1,0:T(8,128)S(1)}, f32[2,8,128]{2,1,0:T(8,128)}, u32[]{:S(2)}) copy-start(f32[2,8,128]{2,1,0:T(8,128)} %param.2) | copy-start | bytes 24580
  1.6 7.6 %collective-permute-start = (f32[136,128]{1,0:T(8,128)S(1)}, f32[136,128]{1,0:T(8,128)S(1)}, u32[]{:S(2)}, u32[]{:S(2)}) collective-permute-start(f32[136,128]{1,0:T(8,128)S(1)} %get-tuple-element.16), channel_id=1, source_target_pairs={{0,4},{4,8},{8,12},{12,0},{1,5},{5,9},{9,13},{13,1},{2,6},{6,10},{... | collective-permute-start | bytes 208904 | tf_op jit(solution)/shard_map/ppermute | solution.py:403
  4.7 5.1 %collective-permute-start.1 = (f32[136,128]{1,0:T(8,128)S(1)}, f32[136,128]{1,0:T(8,128)S(1)}, u32[]{:S(2)}, u32[]{:S(2)}) collective-permute-start(f32[136,128]{1,0:T(8,128)S(1)} %get-tuple-element.17), channel_id=1, source_target_pairs={{0,12},{4,0},{8,4},{12,8},{1,13},{5,1},{9,5},{13,9},{2,14},{6,2},{... | collective-permute-start | bytes 208904 | tf_op jit(solution)/shard_map/ppermute | solution.py:403
  10.5 1.2 %collective-permute-start.2 = (f32[72,128]{1,0:T(8,128)S(1)}, f32[72,128]{1,0:T(8,128)S(1)}, u32[]{:S(2)}, u32[]{:S(2)}) collective-permute-start(f32[72,128]{1,0:T(8,128)S(1)} %get-tuple-element.21.refs_0_), channel_id=1, source_target_pairs={{0,1},{1,0},{2,3},{3,2},{4,5},{5,4},{6,7},{7,6},{8,9},{9,8},{10,11... | collective-permute-start | bytes 110600 | tf_op jit(solution)/shard_map/ppermute | solution.py:403
  12.2 3.5 %collective-permute-start.3 = (f32[72,128]{1,0:T(8,128)S(1)}, f32[72,128]{1,0:T(8,128)S(1)}, u32[]{:S(2)}, u32[]{:S(2)}) collective-permute-start(f32[72,128]{1,0:T(8,128)S(1)} %get-tuple-element.22.refs_0_), channel_id=1, source_target_pairs={{0,3},{1,2},{2,1},{3,0},{4,7},{5,6},{6,5},{7,4},{8,11},{9,10},{10,... | collective-permute-start | bytes 110600 | tf_op jit(solution)/shard_map/ppermute | solution.py:403
  16.3 3.0 %collective-permute-start.4 = (f32[8,128]{1,0:T(8,128)S(1)}, f32[8,128]{1,0:T(8,128)S(1)}, u32[]{:S(2)}, u32[]{:S(2)}) collective-permute-start(f32[8,128]{1,0:T(8,128)S(1)} %get-tuple-element.25), channel_id=1, source_target_pairs={{0,5},{1,4},{2,7},{3,6},{4,1},{5,0},{6,3},{7,2},{8,13},{9,12},{10,... | collective-permute-start | bytes 12296 | tf_op jit(solution)/shard_map/ppermute | solution.py:403
  19.4 3.9 %collective-permute-start.5 = (f32[8,128]{1,0:T(8,128)S(1)}, f32[8,128]{1,0:T(8,128)S(1)}, u32[]{:S(2)}, u32[]{:S(2)}) collective-permute-start(f32[8,128]{1,0:T(8,128)S(1)} %add.6), channel_id=1, source_target_pairs={{0,9},{1,8},{2,11},{3,10},{4,13},{5,12},{6,15},{7,14},{8,1},{9,0},... | collective-permute-start | bytes 12296 | tf_op jit(solution)/shard_map/ppermute | solution.py:403

commit v5 on v4

--- a/solution.py
+++ b/solution.py
@@ -171,50 +171,41 @@
 
 
 def row_sets(rows):
-    return tuple(range(2, rows - 2)), (0, 1, rows - 2, rows - 1)
-
-
-def middle_body(sizes, scale, pv, base, evolved, gram, edges, coef):
-    vectors, layers, rows, columns = sizes
-    source = Rows(sizes, pv, base, None, None)
-
-    def edges_of(group):
-        def put(layer, packed):
-            if packed is None:
-                return jnp.zeros((SUB, columns), jnp.float32)
-            at = edge_place(sizes, layer, group)
-            edges[at, :] = packed[: at.size]
-
-        return put
-
-    wanted, _ = row_sets(rows)
-    step_rows(source, wanted, range(rows), edges_of, evolved, coef)
-    edges[pl.ds(layers * (vectors + 1), SUB - layers), :] = jnp.zeros((SUB - layers, columns), jnp.float32)
-    local = gram_of(evolved[...], scale)
-    for at in range(0, vectors, SUB):
-        gram[pl.ds(at, SUB), :] = at_end(local[at : at + SUB], columns)
-
-
-def border_body(sizes, scale, pv, base, above, below, gram, edges, evolved, message, coef):
-    vectors, layers, rows, columns = sizes
-    source = Rows(sizes, pv, base, above, below)
-    halo = (-2, -1, rows, rows + 1)
+    return tuple(range(2, rows - 2)), (0, 1), (rows - 2, rows - 1)
+
+
+def rows_body(sizes, scale, wanted, edge_rows, below_only, pv, base, *refs):
+    vectors, layers, _, columns = sizes
+    refs = list(refs)
+    halo = refs.pop(0) if below_only is not None else None
+    before = [refs.pop(0), refs.pop(0)] if below_only is not None else None
+    evolved, gram, edges, coef = refs if below_only is not True else (refs[0], None, refs[1], refs[2])
+    source = Rows(sizes, pv, base, halo, halo)
 
     def edges_of(group):
         def put(layer, packed):
             at = edge_place(sizes, layer, group)
-            if packed is None:
-                return jnp.broadcast_to(edges[at, :], (SUB, columns))
-            message[at, :] = packed[: at.size]
+            if packed is not None:
+                edges[at, :] = packed[: at.size]
+            elif before is None:
+                return jnp.zeros((SUB, columns), jnp.float32)
+            else:
+                return jnp.broadcast_to(before[1][at, :], (SUB, columns))
 
         return put
 
-    _, wanted = row_sets(rows)
-    step_rows(source, wanted, halo, edges_of, evolved, coef)
-    message[pl.ds(layers * (vectors + 1), SUB - layers), :] = jnp.zeros((SUB - layers, columns), jnp.float32)
+    step_rows(source, wanted, edge_rows, edges_of, evolved, coef)
+    edges[pl.ds(layers * (vectors + 1), SUB - layers), :] = jnp.zeros((SUB - layers, columns), jnp.float32)
     local = gram_of(evolved[...], scale)
-    for at in range(0, vectors, SUB):
-        message[pl.ds(at, SUB), :] = message[pl.ds(at, SUB), :] + (gram[pl.ds(at, SUB), :] + at_end(local[at : at + SUB], columns))
+    for first in range(0, vectors, SUB):
+        at = pl.ds(first, SUB)
+        total = at_end(local[first : first + SUB], columns)
+        if before is not None:
+            total = before[0][at, :] + total
+        if gram is not None:
+            gram[at, :] = total
+        else:
+            edges[at, :] = edges[at, :] + total
 
 
 def strip_fields(here, columns):
@@ -305,7 +296,7 @@
         message[...] = total
 
 
-def ready_body(sizes, middle, border, sides, parts):
+def ready_body(sizes, middle, upper_rows, lower_rows, sides, parts):
     vectors, layers, rows, columns = sizes
     lane = lanes_of((SUB * 2, columns))
     at_edge = jnp.logical_or(lane < 2, lane >= columns - 2)
@@ -313,12 +304,12 @@
     pair = 2 * SUB
     for layer in range(layers):
         for row in range(rows):
-            which = 0 if row in sets[0] else 1
+            which = [row in part for part in sets].index(True)
             block = layer * len(sets[which]) + sets[which].index(row)
             for first in range(0, vectors, pair):
                 edge = sides[pl.ds(layer * vectors + first, pair), :]
                 edge = pltpu.roll(edge, -(SPAN * (row + 2) + EDGE) % columns, 1)
-                here = (middle, border)[which][pl.ds(first, pair), pl.ds(block * columns, columns)]
+                here = (middle, upper_rows, lower_rows)[which][pl.ds(first, pair), pl.ds(block * columns, columns)]
                 rest = jnp.where(at_edge, edge, here)
                 for n in range(3):
                     part = rest.astype(jnp.bfloat16)
@@ -339,6 +330,9 @@
         turned = pltpu.roll(packed, (columns - group * vectors) % columns, 1)
         unit = jnp.where(lane - vectors == sub + group * SUB, 1.0, 0.0)
         work.append(jnp.where(lane < vectors, turned, unit))
+    order = ((0, 0), (1, 0), (2, 0), (0, 1), (1, 1), (0, 2))
+    per = columns // vectors
+    inverse = []
     for home in range(groups):
         first = home * SUB
         column = {
@@ -346,9 +340,11 @@
             for group in range(home, groups)
             for j in range(SUB)
         }
+        root = jnp.ones(shape, jnp.float32)
         for at in range(SUB):
             inverse_pivot = jnp.broadcast_to((1.0 / column[home, at])[at : at + 1, :], shape)
             line = jnp.broadcast_to(work[home][at : at + 1, :], shape)
+            root = jnp.where(sub == at, column[home, at], root)
             for group in range(home, groups):
                 factor = column[group, at] * inverse_pivot
                 if group == home:
@@ -362,20 +358,13 @@
                 work[group] = work[group] - factor * line
             for j in range(at + 1, SUB):
                 column[home, j] = column.pop((home, j, "next"))
-    order = ((0, 0), (1, 0), (2, 0), (0, 1), (1, 1), (0, 2))
-    slot = lane // vectors
-    inverse = []
-    for group in range(groups):
-        row = sub + group * SUB
-        pivot = jnp.sum(jnp.where(lane == row, work[group], 0.0), axis=1, keepdims=True)
-        done = work[group] * (1.0 / jnp.sqrt(jnp.broadcast_to(pivot, shape)))
-        upper[pl.ds(group * SUB, SUB), :] = jnp.where(lane >= row, done, 0.0)[:, :vectors]
-        rest, terms = jnp.where(slot == 1, done, 0.0), []
+        scaled = work[home] * (1.0 / jnp.sqrt(root))
+        upper[pl.ds(home * SUB, SUB), :] = jnp.where(lane >= sub + home * SUB, scaled, 0.0)[:, :vectors]
+        rest, terms = jnp.where(lane // vectors == 1, scaled, 0.0), []
         for _ in range(3):
             term = rest.astype(jnp.bfloat16).astype(jnp.float32)
             rest = rest - term
             terms.append(term)
-        per = columns // vectors
         wide = []
         for first in range(0, len(order), per):
             line = jnp.zeros(shape, jnp.float32)
@@ -384,8 +373,9 @@
             wide.append(line)
         inverse.append(jnp.concatenate(wide, axis=1))
     inverse = jnp.concatenate(inverse, axis=0).astype(jnp.bfloat16)[:, : len(order) * vectors]
+    wide = 2 if rows % 2 == 0 else 1
+    flat = basis
     stride = layers * rows
-    wide = 2 if stride % 2 == 0 else 1
     for first in range(0, stride, wide):
         at = pl.ds(first * columns, wide * columns)
         split = [parts[pl.ds(n * vectors, vectors), at] for n in range(3)]
@@ -395,7 +385,7 @@
         for n in range(wide):
             for group in range(groups):
                 at = pl.ds(group * SUB * stride + first + n, SUB, stride=stride)
-                basis[at, :] = part[group * SUB : (group + 1) * SUB, n * columns : (n + 1) * columns]
+                flat[at, :] = part[group * SUB : (group + 1) * SUB, n * columns : (n + 1) * columns]
 
 
 def exchange(value, axis, partner):
@@ -414,12 +404,12 @@
     base = base_stream.reshape(layers * rows, columns)
     f32 = lambda *shape: jax.ShapeDtypeStruct(shape, jnp.float32)
 
-    def call(body, outs, *operands, scratch=(), inputs=VMEM):
+    def call(body, outs, *operands, scratch=(), inputs=VMEM, first_out=VMEM):
         return pl.pallas_call(
             lambda *refs: body(sizes, *refs),
             out_shape=outs,
             in_specs=[inputs] * len(operands),
-            out_specs=[VMEM] * len(outs),
+            out_specs=[first_out] + [VMEM] * (len(outs) - 1),
             scratch_shapes=scratch,
             compiler_params=pltpu.CompilerParams(vmem_limit_bytes=8 << 20),
         )(*operands)
@@ -441,19 +431,20 @@
     cells = layers * rows * columns
     scale = 1.0 / (cells * down * across)
     parcel = f32(layers * vectors + SUB, columns)
-    middle_rows, border_rows = (layers * len(part) for part in row_sets(rows))
-    middle, gram, edges = call(
-        lambda sizes, *refs: middle_body(sizes, scale, *refs),
-        [f32(vectors, middle_rows * columns), f32(vectors, columns), parcel],
-        pv, base,
-        scratch=[pltpu.VMEM((middle_rows, 4, SUB, columns), jnp.float32)],
-    )
-    border, message = call(
-        lambda sizes, *refs: border_body(sizes, scale, *refs),
-        [f32(vectors, border_rows * columns), parcel],
-        pv, base, above, below, gram, edges,
-        scratch=[pltpu.VMEM((border_rows, 4, SUB, columns), jnp.float32)],
-    )
+    middle_set, upper_set, lower_set = row_sets(rows)
+
+    def rows_call(wanted, edge_rows, below_only, *operands):
+        blocks = layers * len(wanted)
+        return call(
+            lambda sizes, *refs: rows_body(sizes, scale, wanted, edge_rows, below_only, *refs),
+            [f32(vectors, blocks * columns)] + [f32(vectors, columns)] * (below_only is not True) + [parcel],
+            pv, base, *operands,
+            scratch=[pltpu.VMEM((blocks, 4, SUB, columns), jnp.float32)],
+        )
+
+    middle, gram, edges = rows_call(middle_set, range(rows), None)
+    upper_rows, gram, edges = rows_call(upper_set, (-2, -1), False, above, gram, edges)
+    lower_rows, message = rows_call(lower_set, (rows, rows + 1), True, below, gram, edges)
     half, sides = 1, ()
     while half < across:
         last = 2 * half == across
@@ -466,7 +457,7 @@
             scratch=[pltpu.VMEM((vectors, (2 if last else 1) * layers * columns), jnp.float32)],
         )
         half *= 2
-    (parts,) = call(ready_body, [jax.ShapeDtypeStruct((3 * vectors, cells), jnp.bfloat16)], middle, border, *sides)
+    (parts,) = call(ready_body, [jax.ShapeDtypeStruct((3 * vectors, cells), jnp.bfloat16)], middle, upper_rows, lower_rows, *sides)
     gram = message
     half = 1
     while half < down:

time: 25.3 us -> 25 us (0.988)
  waiting for transfers between devices: 10.1 us -> 9.4 us
    ppermute x6, waiting for transfers between devices: 10.1 us -> 9.4 us  [exchange(): return lax.ppermute(value, axis, [(i, partner(i)) for i in range(count)])]
    pallas_call x7 -> x8, Pallas kernels: 5.28 us -> 5.53 us  [call(): pl.pallas_call(lambda *refs: body(sizes, *refs), out_shape=outs, in_specs...]
  transfers between devices with their start and end apart: 6 -> 6, of which waited for: 6 -> 6; matrix products, arithmetic and copies ran while one was open for 0% -> 0% of each run, Pallas kernels for 3% -> 5%
where the time goes in v5:
time: 25 us; the launch traced here: 24.9 us
  waiting for transfers between devices  9.4 us (38%)
  starting transfers between devices  9.27 us (37%)
  Pallas kernels  5.53 us (22%)
  between operations  0.68 us (3%)
    ppermute x6, waiting for transfers between devices, exchange(): return lax.ppermute(value, axis, [(i, partner(i)) for i in range(count)])  9.4 us
    ppermute x6, starting transfers between devices, exchange(): return lax.ppermute(value, axis, [(i, partner(i)) for i in range(count)])  9.27 us
    pallas_call x8, Pallas kernels, call(): pl.pallas_call(lambda *refs: body(sizes, *refs), out_shape=outs, in_specs...  5.53 us
  transfers between devices with their start and end apart: 6, of which 6 were waited for; matrix products, arithmetic and copies ran while one was open for 0% of the time, Pallas kernels for 5%

profile of v5, /device:TPU:0, one launch (start us, length us, event | category | flops | bytes accessed | tf_op | source)
XLA Modules:
  0.0 24.9 jit_solution(577963048701065859)
XLA Ops:
  0.6 0.0 copy-start
  0.6 0.0 copy-start.1
  0.6 1.0 %shard_map.42 = (f32[136,128]{1,0:T(8,128)S(1)}, f32[136,128]{1,0:T(8,128)S(1)}) custom-call(f32[64,8,128]{2,1,0:T(8,128)} %bitcast.4, f32[16,128]{1,0:T(8,128)} %bitcast.8), custom_call_target="tpu_custom_call" | custom-call | tf_op jit(solution)/shard_map/pallas_call | solution.py:408
  1.6 3.1 %collective-permute-start = (f32[136,128]{1,0:T(8,128)S(1)}, f32[136,128]{1,0:T(8,128)S(1)}, u32[]{:S(2)}, u32[]{:S(2)}) collective-permute-start(f32[136,128]{1,0:T(8,128)S(1)} %get-tuple-element.19), channel_id=1, source_target_pairs={{0,4},{4,8},{8,12},{12,0},{1,5},{5,9},{9,13},{13,1},{2,6},{6,10},{... | collective-permute-start | bytes 208904 | tf_op jit(solution)/shard_map/ppermute | solution.py:393
  4.7 2.1 %collective-permute-start.1 = (f32[136,128]{1,0:T(8,128)S(1)}, f32[136,128]{1,0:T(8,128)S(1)}, u32[]{:S(2)}, u32[]{:S(2)}) collective-permute-start(f32[136,128]{1,0:T(8,128)S(1)} %get-tuple-element.23), channel_id=1, source_target_pairs={{0,12},{4,0},{8,4},{12,8},{1,13},{5,1},{9,5},{13,9},{2,14},{6,2},{... | collective-permute-start | bytes 208904 | tf_op jit(solution)/shard_map/ppermute | solution.py:393
  6.8 0.0 copy-done
  6.8 0.0 copy-done.1
  6.8 0.6 %shard_map.41 = (f32[32,1024]{1,0:T(8,128)S(1)}, f32[32,128]{1,0:T(8,128)S(1)}, f32[72,128]{1,0:T(8,128)S(1)}) custom-call(f32[512,128]{1,0:T(8,128)S(1)} %bitcast.5, f32[16,128]{1,0:T(8,128)S(1)} %bitcast.9), custom_call_target="tpu_custom_call" | custom-call | tf_op jit(solution)/shard_map/pallas_call | solution.py:408
  7.5 1.7 %collective-permute-done.refs_2_ = f32[136,128]{1,0:T(8,128)S(1)} collective-permute-done((f32[136,128]{1,0:T(8,128)S(1)}, f32[136,128]{1,0:T(8,128)S(1)}, u32[]{:S(2)}, u32[]{:S(2)}) %collective-permute-start) | collective-permute-done | bytes 69664 | tf_op jit(solution)/shard_map/ppermute | solution.py:393
  9.2 0.5 %shard_map.43 = (f32[32,512]{1,0:T(8,128)S(1)}, f32[32,128]{1,0:T(8,128)S(1)}, f32[72,128]{1,0:T(8,128)S(1)}) custom-call(f32[512,128]{1,0:T(8,128)S(1)} %bitcast.6, f32[16,128]{1,0:T(8,128)S(1)} %bitcast.10, f32[136,128]{1,0:T(8,128)S(1)} %collective-permute-done.refs_2_, f32[32,128]{1,0:T(8,128)S(1)} %get-tuple-element.20.refs_3_, ...), custom_call_target="tpu_custom_call" | custom-call | tf_op jit(solution)/shard_map/pallas_call | solution.py:408
  9.7 0.2 collective-permute-done.1.refs_2_
  9.9 0.5 %shard_map.44 = (f32[32,512]{1,0:T(8,128)S(1)}, f32[72,128]{1,0:T(8,128)S(1)}) custom-call(f32[512,128]{1,0:T(8,128)S(1)} %bitcast.7, f32[16,128]{1,0:T(8,128)S(1)} %bitcast.11, f32[136,128]{1,0:T(8,128)S(1)} %collective-permute-done.1.refs_2_, f32[32,128]{1,0:T(8,128)S(1)} %get-tuple-element.24.refs_3_, f32[72,128]{1,0:T(8,128)S(1)} %get-tuple-element.25.refs_4_), custom_call_target="tpu_custom_call" | custom-call | tf_op jit(solution)/shard_map/pallas_call | solution.py:408
  10.3 0.0 collective-permute-start.2
  10.4 1.2 %collective-permute-done.2.refs_1_ = f32[72,128]{1,0:T(8,128)S(1)} collective-permute-done((f32[72,128]{1,0:T(8,128)S(1)}, f32[72,128]{1,0:T(8,128)S(1)}, u32[]{:S(2)}, u32[]{:S(2)}) %collective-permute-start.2) | collective-permute-done | bytes 36896 | tf_op jit(solution)/shard_map/ppermute | solution.py:393
  11.6 0.4 %shard_map.45 = (f32[72,128]{1,0:T(8,128)S(1)}, f32[64,128]{1,0:T(8,128)S(1)}) custom-call(f32[72,128]{1,0:T(8,128)S(1)} %get-tuple-element.27.refs_0_, f32[72,128]{1,0:T(8,128)S(1)} %collective-permute-done.2.refs_1_), custom_call_target="tpu_custom_call" | custom-call | tf_op jit(solution)/shard_map/pallas_call | solution.py:408
  12.0 1.5 %collective-permute-start.3 = (f32[72,128]{1,0:T(8,128)S(1)}, f32[72,128]{1,0:T(8,128)S(1)}, u32[]{:S(2)}, u32[]{:S(2)}) collective-permute-start(f32[72,128]{1,0:T(8,128)S(1)} %get-tuple-element.28.refs_0_), channel_id=1, source_target_pairs={{0,3},{1,2},{2,1},{3,0},{4,7},{5,6},{6,5},{7,4},{8,11},{9,10},{10,... | collective-permute-start | bytes 110600 | tf_op jit(solution)/shard_map/ppermute | solution.py:393
  13.5 1.9 %collective-permute-done.3.refs_1_ = f32[72,128]{1,0:T(8,128)S(1)} collective-permute-done((f32[72,128]{1,0:T(8,128)S(1)}, f32[72,128]{1,0:T(8,128)S(1)}, u32[]{:S(2)}, u32[]{:S(2)}) %collective-permute-start.3) | collective-permute-done | bytes 36896 | tf_op jit(solution)/shard_map/ppermute | solution.py:393
  15.5 0.7 %shard_map.46 = (f32[8,128]{1,0:T(8,128)S(1)}, f32[64,128]{1,0:T(8,128)S(1)}) custom-call(f32[72,128]{1,0:T(8,128)S(1)} %get-tuple-element.28.refs_0_, f32[72,128]{1,0:T(8,128)S(1)} %collective-permute-done.3.refs_1_, f32[64,128]{1,0:T(8,128)S(1)} %get-tuple-element.29.refs_2_), custom_call_target="tpu_custom_call" | custom-call | tf_op jit(solution)/shard_map/pallas_call | solution.py:408
  16.1 0.9 %collective-permute-start.4 = (f32[8,128]{1,0:T(8,128)S(1)}, f32[8,128]{1,0:T(8,128)S(1)}, u32[]{:S(2)}, u32[]{:S(2)}) collective-permute-start(f32[8,128]{1,0:T(8,128)S(1)} %get-tuple-element.31), channel_id=1, source_target_pairs={{0,5},{1,4},{2,7},{3,6},{4,1},{5,0},{6,3},{7,2},{8,13},{9,12},{10,... | collective-permute-start | bytes 12296 | tf_op jit(solution)/shard_map/ppermute | solution.py:393
  17.0 2.1 %collective-permute-done.4 = f32[8,128]{1,0:T(8,128)S(1)} collective-permute-done((f32[8,128]{1,0:T(8,128)S(1)}, f32[8,128]{1,0:T(8,128)S(1)}, u32[]{:S(2)}, u32[]{:S(2)}) %collective-permute-start.4) | collective-permute-done | bytes 4128 | tf_op jit(solution)/shard_map/ppermute | solution.py:393
  19.2 1.6 %collective-permute-start.5 = (f32[8,128]{1,0:T(8,128)S(1)}, f32[8,128]{1,0:T(8,128)S(1)}, u32[]{:S(2)}, u32[]{:S(2)}) collective-permute-start(f32[8,128]{1,0:T(8,128)S(1)} %add.6), channel_id=1, source_target_pairs={{0,9},{1,8},{2,11},{3,10},{4,13},{5,12},{6,15},{7,14},{8,1},{9,0},... | collective-permute-start | bytes 12296 | tf_op jit(solution)/shard_map/ppermute | solution.py:393
  20.8 0.2 shard_map.47.refs_0_
  21.0 2.2 %collective-permute-done.5 = f32[8,128]{1,0:T(8,128)S(1)} collective-permute-done((f32[8,128]{1,0:T(8,128)S(1)}, f32[8,128]{1,0:T(8,128)S(1)}, u32[]{:S(2)}, u32[]{:S(2)}) %collective-permute-start.5) | collective-permute-done | bytes 4128 | tf_op jit(solution)/shard_map/ppermute | solution.py:393
  23.1 1.8 %shard_map.48 = (f32[512,128]{1,0:T(8,128)}, f32[32,32]{1,0:T(8,128)}) custom-call(bf16[96,2048]{1,0:T(8,128)(2,1)S(1)} %shard_map.47.refs_0_, f32[8,128]{1,0:T(8,128)S(1)} %add.7.refs_1_), custom_call_target="tpu_custom_call" | custom-call | tf_op jit(solution)/shard_map/pallas_call | solution.py:408
  (2 shorter events, 0.0 us)
Async XLA Ops:
  0.6 6.2 %copy-start = (f32[32,2,8,128]{3,2,1,0:T(8,128)S(1)}, f32[32,2,8,128]{3,2,1,0:T(8,128)}, u32[]{:S(2)}) copy-start(f32[32,2,8,128]{3,2,1,0:T(8,128)} %param.3) | copy-start | bytes 786436
  0.6 6.2 %copy-start.1 = (f32[2,8,128]{2,1,0:T(8,128)S(1)}, f32[2,8,128]{2,1,0:T(8,128)}, u32[]{:S(2)}) copy-start(f32[2,8,128]{2,1,0:T(8,128)} %param.2) | copy-start | bytes 24580
  1.6 7.6 %collective-permute-start = (f32[136,128]{1,0:T(8,128)S(1)}, f32[136,128]{1,0:T(8,128)S(1)}, u32[]{:S(2)}, u32[]{:S(2)}) collective-permute-start(f32[136,128]{1,0:T(8,128)S(1)} %get-tuple-element.19), channel_id=1, source_target_pairs={{0,4},{4,8},{8,12},{12,0},{1,5},{5,9},{9,13},{13,1},{2,6},{6,10},{... | collective-permute-start | bytes 208904 | tf_op jit(solution)/shard_map/ppermute | solution.py:393
  4.7 5.1 %collective-permute-start.1 = (f32[136,128]{1,0:T(8,128)S(1)}, f32[136,128]{1,0:T(8,128)S(1)}, u32[]{:S(2)}, u32[]{:S(2)}) collective-permute-start(f32[136,128]{1,0:T(8,128)S(1)} %get-tuple-element.23), channel_id=1, source_target_pairs={{0,12},{4,0},{8,4},{12,8},{1,13},{5,1},{9,5},{13,9},{2,14},{6,2},{... | collective-permute-start | bytes 208904 | tf_op jit(solution)/shard_map/ppermute | solution.py:393
  10.3 1.2 %collective-permute-start.2 = (f32[72,128]{1,0:T(8,128)S(1)}, f32[72,128]{1,0:T(8,128)S(1)}, u32[]{:S(2)}, u32[]{:S(2)}) collective-permute-start(f32[72,128]{1,0:T(8,128)S(1)} %get-tuple-element.27.refs_0_), channel_id=1, source_target_pairs={{0,1},{1,0},{2,3},{3,2},{4,5},{5,4},{6,7},{7,6},{8,9},{9,8},{10,11... | collective-permute-start | bytes 110600 | tf_op jit(solution)/shard_map/ppermute | solution.py:393
  12.0 3.5 %collective-permute-start.3 = (f32[72,128]{1,0:T(8,128)S(1)}, f32[72,128]{1,0:T(8,128)S(1)}, u32[]{:S(2)}, u32[]{:S(2)}) collective-permute-start(f32[72,128]{1,0:T(8,128)S(1)} %get-tuple-element.28.refs_0_), channel_id=1, source_target_pairs={{0,3},{1,2},{2,1},{3,0},{4,7},{5,6},{6,5},{7,4},{8,11},{9,10},{10,... | collective-permute-start | bytes 110600 | tf_op jit(solution)/shard_map/ppermute | solution.py:393
  16.1 3.0 %collective-permute-start.4 = (f32[8,128]{1,0:T(8,128)S(1)}, f32[8,128]{1,0:T(8,128)S(1)}, u32[]{:S(2)}, u32[]{:S(2)}) collective-permute-start(f32[8,128]{1,0:T(8,128)S(1)} %get-tuple-element.31), channel_id=1, source_target_pairs={{0,5},{1,4},{2,7},{3,6},{4,1},{5,0},{6,3},{7,2},{8,13},{9,12},{10,... | collective-permute-start | bytes 12296 | tf_op jit(solution)/shard_map/ppermute | solution.py:393
  19.2 3.9 %collective-permute-start.5 = (f32[8,128]{1,0:T(8,128)S(1)}, f32[8,128]{1,0:T(8,128)S(1)}, u32[]{:S(2)}, u32[]{:S(2)}) collective-permute-start(f32[8,128]{1,0:T(8,128)S(1)} %add.6), channel_id=1, source_target_pairs={{0,9},{1,8},{2,11},{3,10},{4,13},{5,12},{6,15},{7,14},{8,1},{9,0},... | collective-permute-start | bytes 12296 | tf_op jit(solution)/shard_map/ppermute | solution.py:393

commit v6 on v5

--- a/solution.py
+++ b/solution.py
@@ -282,18 +282,19 @@
     if not last:
         message[pl.ds(layers * (vectors + 1), SUB - layers), :] = jnp.zeros((SUB - layers, columns), jnp.float32)
     local = gram_of(strips[...], scale)
-    total = jnp.zeros(shape, jnp.float32)
     free = columns - vectors
-    for group in range(groups):
-        block = pl.ds(group * SUB, SUB)
-        joined = parcel[group] + at_end(local[group * SUB : (group + 1) * SUB], columns)
-        if last:
-            turned = pltpu.roll(joined, (vectors * (group + 1)) % columns, 1) if group + 1 < groups else joined
+    if last:
+        total = jnp.zeros(shape, jnp.float32)
+        for group in range(groups):
+            turned = pltpu.roll(parcel[group], vectors * (group + 1) % columns, 1)
             total = jnp.where(lane // vectors == group, turned, total)
-        else:
+        packed = jnp.concatenate([local[at : at + SUB] for at in range(0, vectors, SUB)], axis=1)
+        message[...] = total + packed
+    else:
+        for group in range(groups):
+            block = pl.ds(group * SUB, SUB)
+            joined = parcel[group] + at_end(local[group * SUB : (group + 1) * SUB], columns)
             message[block, :] = jnp.where(lane >= free, joined, message[block, :])
-    if last:
-        message[...] = total
 
 
 def ready_body(sizes, middle, upper_rows, lower_rows, sides, parts):
@@ -333,31 +334,31 @@
     order = ((0, 0), (1, 0), (2, 0), (0, 1), (1, 1), (0, 2))
     per = columns // vectors
     inverse = []
+    column = {}
+
+    def spread(panel, above):
+        for j in range(panel * SUB, (panel + 1) * SUB):
+            for group in range(above, groups):
+                column[group, j] = jnp.broadcast_to(work[group][:, j : j + 1], shape)
+
+    spread(0, 0)
     for home in range(groups):
-        first = home * SUB
-        column = {
-            (group, j): jnp.broadcast_to(work[group][:, first + j : first + j + 1], shape)
-            for group in range(home, groups)
-            for j in range(SUB)
-        }
+        if home + 1 < groups:
+            spread(home + 1, home)
         root = jnp.ones(shape, jnp.float32)
         for at in range(SUB):
-            inverse_pivot = jnp.broadcast_to((1.0 / column[home, at])[at : at + 1, :], shape)
+            k = home * SUB + at
+            inverse_pivot = jnp.broadcast_to((1.0 / column[home, k])[at : at + 1, :], shape)
             line = jnp.broadcast_to(work[home][at : at + 1, :], shape)
-            root = jnp.where(sub == at, column[home, at], root)
+            root = jnp.where(sub == at, column[home, k], root)
+            factor = {group: column[group, k] * inverse_pivot for group in range(home, groups)}
+            factor[home] = jnp.where(sub > at, factor[home], 0.0)
+            for j in range(k + 1, min((home + 2) * SUB, vectors)):
+                level = jnp.broadcast_to(column[home, j][at : at + 1, :], shape)
+                for group in range(home, groups):
+                    column[group, j] = column[group, j] - factor[group] * level
             for group in range(home, groups):
-                factor = column[group, at] * inverse_pivot
-                if group == home:
-                    factor = jnp.where(sub > at, factor, 0.0)
-                for j in range(at + 1, SUB):
-                    level = jnp.broadcast_to(column[home, j][at : at + 1, :], shape)
-                    if group == home:
-                        column[home, j, "next"] = column[home, j] - factor * level
-                    else:
-                        column[group, j] = column[group, j] - factor * level
-                work[group] = work[group] - factor * line
-            for j in range(at + 1, SUB):
-                column[home, j] = column.pop((home, j, "next"))
+                work[group] = work[group] - factor[group] * line
         scaled = work[home] * (1.0 / jnp.sqrt(root))
         upper[pl.ds(home * SUB, SUB), :] = jnp.where(lane >= sub + home * SUB, scaled, 0.0)[:, :vectors]
         rest, terms = jnp.where(lane // vectors == 1, scaled, 0.0), []

time: 25 us -> 24.8 us (level)
  no operation moved by 1% of the time
where the time goes in v6:
time: 24.8 us; the launch traced here: 24.7 us
  waiting for transfers between devices  9.4 us (38%)
  starting transfers between devices  9.27 us (37%)
  Pallas kernels  5.32 us (21%)
  between operations  0.68 us (3%)
    ppermute x6, waiting for transfers between devices, exchange(): return lax.ppermute(value, axis, [(i, partner(i)) for i in range(count)])  9.4 us
    ppermute x6, starting transfers between devices, exchange(): return lax.ppermute(value, axis, [(i, partner(i)) for i in range(count)])  9.27 us
    pallas_call x8, Pallas kernels, call(): pl.pallas_call(lambda *refs: body(sizes, *refs), out_shape=outs, in_specs...  5.32 us
  transfers between devices with their start and end apart: 6, of which 6 were waited for; matrix products, arithmetic and copies ran while one was open for 0% of the time, Pallas kernels for 5%

profile of v6, /device:TPU:0, one launch (start us, length us, event | category | flops | bytes accessed | tf_op | source)
XLA Modules:
  0.0 24.7 jit_solution(11204353625660860101)
XLA Ops:
  0.6 0.0 copy-start
  0.6 0.0 copy-start.1
  0.6 1.0 %shard_map.42 = (f32[136,128]{1,0:T(8,128)S(1)}, f32[136,128]{1,0:T(8,128)S(1)}) custom-call(f32[64,8,128]{2,1,0:T(8,128)} %bitcast.4, f32[16,128]{1,0:T(8,128)} %bitcast.8), custom_call_target="tpu_custom_call" | custom-call | tf_op jit(solution)/shard_map/pallas_call | solution.py:409
  1.6 3.1 %collective-permute-start = (f32[136,128]{1,0:T(8,128)S(1)}, f32[136,128]{1,0:T(8,128)S(1)}, u32[]{:S(2)}, u32[]{:S(2)}) collective-permute-start(f32[136,128]{1,0:T(8,128)S(1)} %get-tuple-element.19), channel_id=1, source_target_pairs={{0,4},{4,8},{8,12},{12,0},{1,5},{5,9},{9,13},{13,1},{2,6},{6,10},{... | collective-permute-start | bytes 208904 | tf_op jit(solution)/shard_map/ppermute | solution.py:394
  4.7 2.1 %collective-permute-start.1 = (f32[136,128]{1,0:T(8,128)S(1)}, f32[136,128]{1,0:T(8,128)S(1)}, u32[]{:S(2)}, u32[]{:S(2)}) collective-permute-start(f32[136,128]{1,0:T(8,128)S(1)} %get-tuple-element.23), channel_id=1, source_target_pairs={{0,12},{4,0},{8,4},{12,8},{1,13},{5,1},{9,5},{13,9},{2,14},{6,2},{... | collective-permute-start | bytes 208904 | tf_op jit(solution)/shard_map/ppermute | solution.py:394
  6.8 0.0 copy-done
  6.8 0.0 copy-done.1
  6.8 0.6 %shard_map.41 = (f32[32,1024]{1,0:T(8,128)S(1)}, f32[32,128]{1,0:T(8,128)S(1)}, f32[72,128]{1,0:T(8,128)S(1)}) custom-call(f32[512,128]{1,0:T(8,128)S(1)} %bitcast.5, f32[16,128]{1,0:T(8,128)S(1)} %bitcast.9), custom_call_target="tpu_custom_call" | custom-call | tf_op jit(solution)/shard_map/pallas_call | solution.py:409
  7.5 1.7 %collective-permute-done.refs_2_ = f32[136,128]{1,0:T(8,128)S(1)} collective-permute-done((f32[136,128]{1,0:T(8,128)S(1)}, f32[136,128]{1,0:T(8,128)S(1)}, u32[]{:S(2)}, u32[]{:S(2)}) %collective-permute-start) | collective-permute-done | bytes 69664 | tf_op jit(solution)/shard_map/ppermute | solution.py:394
  9.2 0.5 %shard_map.43 = (f32[32,512]{1,0:T(8,128)S(1)}, f32[32,128]{1,0:T(8,128)S(1)}, f32[72,128]{1,0:T(8,128)S(1)}) custom-call(f32[512,128]{1,0:T(8,128)S(1)} %bitcast.6, f32[16,128]{1,0:T(8,128)S(1)} %bitcast.10, f32[136,128]{1,0:T(8,128)S(1)} %collective-permute-done.refs_2_, f32[32,128]{1,0:T(8,128)S(1)} %get-tuple-element.20.refs_3_, ...), custom_call_target="tpu_custom_call" | custom-call | tf_op jit(solution)/shard_map/pallas_call | solution.py:409
  9.7 0.2 collective-permute-done.1.refs_2_
  9.9 0.5 %shard_map.44 = (f32[32,512]{1,0:T(8,128)S(1)}, f32[72,128]{1,0:T(8,128)S(1)}) custom-call(f32[512,128]{1,0:T(8,128)S(1)} %bitcast.7, f32[16,128]{1,0:T(8,128)S(1)} %bitcast.11, f32[136,128]{1,0:T(8,128)S(1)} %collective-permute-done.1.refs_2_, f32[32,128]{1,0:T(8,128)S(1)} %get-tuple-element.24.refs_3_, f32[72,128]{1,0:T(8,128)S(1)} %get-tuple-element.25.refs_4_), custom_call_target="tpu_custom_call" | custom-call | tf_op jit(solution)/shard_map/pallas_call | solution.py:409
  10.3 0.0 collective-permute-start.2
  10.4 1.2 %collective-permute-done.2.refs_1_ = f32[72,128]{1,0:T(8,128)S(1)} collective-permute-done((f32[72,128]{1,0:T(8,128)S(1)}, f32[72,128]{1,0:T(8,128)S(1)}, u32[]{:S(2)}, u32[]{:S(2)}) %collective-permute-start.2) | collective-permute-done | bytes 36896 | tf_op jit(solution)/shard_map/ppermute | solution.py:394
  11.6 0.4 %shard_map.45 = (f32[72,128]{1,0:T(8,128)S(1)}, f32[64,128]{1,0:T(8,128)S(1)}) custom-call(f32[72,128]{1,0:T(8,128)S(1)} %get-tuple-element.27.refs_0_, f32[72,128]{1,0:T(8,128)S(1)} %collective-permute-done.2.refs_1_), custom_call_target="tpu_custom_call" | custom-call | tf_op jit(solution)/shard_map/pallas_call | solution.py:409
  12.0 1.5 %collective-permute-start.3 = (f32[72,128]{1,0:T(8,128)S(1)}, f32[72,128]{1,0:T(8,128)S(1)}, u32[]{:S(2)}, u32[]{:S(2)}) collective-permute-start(f32[72,128]{1,0:T(8,128)S(1)} %get-tuple-element.28.refs_0_), channel_id=1, source_target_pairs={{0,3},{1,2},{2,1},{3,0},{4,7},{5,6},{6,5},{7,4},{8,11},{9,10},{10,... | collective-permute-start | bytes 110600 | tf_op jit(solution)/shard_map/ppermute | solution.py:394
  13.5 1.9 %collective-permute-done.3.refs_1_ = f32[72,128]{1,0:T(8,128)S(1)} collective-permute-done((f32[72,128]{1,0:T(8,128)S(1)}, f32[72,128]{1,0:T(8,128)S(1)}, u32[]{:S(2)}, u32[]{:S(2)}) %collective-permute-start.3) | collective-permute-done | bytes 36896 | tf_op jit(solution)/shard_map/ppermute | solution.py:394
  15.5 0.6 %shard_map.46 = (f32[8,128]{1,0:T(8,128)S(1)}, f32[64,128]{1,0:T(8,128)S(1)}) custom-call(f32[72,128]{1,0:T(8,128)S(1)} %get-tuple-element.28.refs_0_, f32[72,128]{1,0:T(8,128)S(1)} %collective-permute-done.3.refs_1_, f32[64,128]{1,0:T(8,128)S(1)} %get-tuple-element.29.refs_2_), custom_call_target="tpu_custom_call" | custom-call | tf_op jit(solution)/shard_map/pallas_call | solution.py:409
  16.1 0.9 %collective-permute-start.4 = (f32[8,128]{1,0:T(8,128)S(1)}, f32[8,128]{1,0:T(8,128)S(1)}, u32[]{:S(2)}, u32[]{:S(2)}) collective-permute-start(f32[8,128]{1,0:T(8,128)S(1)} %get-tuple-element.31), channel_id=1, source_target_pairs={{0,5},{1,4},{2,7},{3,6},{4,1},{5,0},{6,3},{7,2},{8,13},{9,12},{10,... | collective-permute-start | bytes 12296 | tf_op jit(solution)/shard_map/ppermute | solution.py:394
  17.0 2.1 %collective-permute-done.4 = f32[8,128]{1,0:T(8,128)S(1)} collective-permute-done((f32[8,128]{1,0:T(8,128)S(1)}, f32[8,128]{1,0:T(8,128)S(1)}, u32[]{:S(2)}, u32[]{:S(2)}) %collective-permute-start.4) | collective-permute-done | bytes 4128 | tf_op jit(solution)/shard_map/ppermute | solution.py:394
  19.1 1.6 %collective-permute-start.5 = (f32[8,128]{1,0:T(8,128)S(1)}, f32[8,128]{1,0:T(8,128)S(1)}, u32[]{:S(2)}, u32[]{:S(2)}) collective-permute-start(f32[8,128]{1,0:T(8,128)S(1)} %add.6), channel_id=1, source_target_pairs={{0,9},{1,8},{2,11},{3,10},{4,13},{5,12},{6,15},{7,14},{8,1},{9,0},... | collective-permute-start | bytes 12296 | tf_op jit(solution)/shard_map/ppermute | solution.py:394
  20.7 0.2 shard_map.47.refs_0_
  20.9 2.2 %collective-permute-done.5 = f32[8,128]{1,0:T(8,128)S(1)} collective-permute-done((f32[8,128]{1,0:T(8,128)S(1)}, f32[8,128]{1,0:T(8,128)S(1)}, u32[]{:S(2)}, u32[]{:S(2)}) %collective-permute-start.5) | collective-permute-done | bytes 4128 | tf_op jit(solution)/shard_map/ppermute | solution.py:394
  23.1 1.6 %shard_map.48 = (f32[512,128]{1,0:T(8,128)}, f32[32,32]{1,0:T(8,128)}) custom-call(bf16[96,2048]{1,0:T(8,128)(2,1)S(1)} %shard_map.47.refs_0_, f32[8,128]{1,0:T(8,128)S(1)} %add.7.refs_1_), custom_call_target="tpu_custom_call" | custom-call | tf_op jit(solution)/shard_map/pallas_call | solution.py:409
  (2 shorter events, 0.0 us)
Async XLA Ops:
  0.6 6.2 %copy-start = (f32[32,2,8,128]{3,2,1,0:T(8,128)S(1)}, f32[32,2,8,128]{3,2,1,0:T(8,128)}, u32[]{:S(2)}) copy-start(f32[32,2,8,128]{3,2,1,0:T(8,128)} %param.3) | copy-start | bytes 786436
  0.6 6.2 %copy-start.1 = (f32[2,8,128]{2,1,0:T(8,128)S(1)}, f32[2,8,128]{2,1,0:T(8,128)}, u32[]{:S(2)}) copy-start(f32[2,8,128]{2,1,0:T(8,128)} %param.2) | copy-start | bytes 24580
  1.6 7.6 %collective-permute-start = (f32[136,128]{1,0:T(8,128)S(1)}, f32[136,128]{1,0:T(8,128)S(1)}, u32[]{:S(2)}, u32[]{:S(2)}) collective-permute-start(f32[136,128]{1,0:T(8,128)S(1)} %get-tuple-element.19), channel_id=1, source_target_pairs={{0,4},{4,8},{8,12},{12,0},{1,5},{5,9},{9,13},{13,1},{2,6},{6,10},{... | collective-permute-start | bytes 208904 | tf_op jit(solution)/shard_map/ppermute | solution.py:394
  4.7 5.1 %collective-permute-start.1 = (f32[136,128]{1,0:T(8,128)S(1)}, f32[136,128]{1,0:T(8,128)S(1)}, u32[]{:S(2)}, u32[]{:S(2)}) collective-permute-start(f32[136,128]{1,0:T(8,128)S(1)} %get-tuple-element.23), channel_id=1, source_target_pairs={{0,12},{4,0},{8,4},{12,8},{1,13},{5,1},{9,5},{13,9},{2,14},{6,2},{... | collective-permute-start | bytes 208904 | tf_op jit(solution)/shard_map/ppermute | solution.py:394
  10.3 1.2 %collective-permute-start.2 = (f32[72,128]{1,0:T(8,128)S(1)}, f32[72,128]{1,0:T(8,128)S(1)}, u32[]{:S(2)}, u32[]{:S(2)}) collective-permute-start(f32[72,128]{1,0:T(8,128)S(1)} %get-tuple-element.27.refs_0_), channel_id=1, source_target_pairs={{0,1},{1,0},{2,3},{3,2},{4,5},{5,4},{6,7},{7,6},{8,9},{9,8},{10,11... | collective-permute-start | bytes 110600 | tf_op jit(solution)/shard_map/ppermute | solution.py:394
  12.0 3.5 %collective-permute-start.3 = (f32[72,128]{1,0:T(8,128)S(1)}, f32[72,128]{1,0:T(8,128)S(1)}, u32[]{:S(2)}, u32[]{:S(2)}) collective-permute-start(f32[72,128]{1,0:T(8,128)S(1)} %get-tuple-element.28.refs_0_), channel_id=1, source_target_pairs={{0,3},{1,2},{2,1},{3,0},{4,7},{5,6},{6,5},{7,4},{8,11},{9,10},{10,... | collective-permute-start | bytes 110600 | tf_op jit(solution)/shard_map/ppermute | solution.py:394
  16.1 3.0 %collective-permute-start.4 = (f32[8,128]{1,0:T(8,128)S(1)}, f32[8,128]{1,0:T(8,128)S(1)}, u32[]{:S(2)}, u32[]{:S(2)}) collective-permute-start(f32[8,128]{1,0:T(8,128)S(1)} %get-tuple-element.31), channel_id=1, source_target_pairs={{0,5},{1,4},{2,7},{3,6},{4,1},{5,0},{6,3},{7,2},{8,13},{9,12},{10,... | collective-permute-start | bytes 12296 | tf_op jit(solution)/shard_map/ppermute | solution.py:394
  19.1 3.9 %collective-permute-start.5 = (f32[8,128]{1,0:T(8,128)S(1)}, f32[8,128]{1,0:T(8,128)S(1)}, u32[]{:S(2)}, u32[]{:S(2)}) collective-permute-start(f32[8,128]{1,0:T(8,128)S(1)} %add.6), channel_id=1, source_target_pairs={{0,9},{1,8},{2,11},{3,10},{4,13},{5,12},{6,15},{7,14},{8,1},{9,0},... | collective-permute-start | bytes 12296 | tf_op jit(solution)/shard_map/ppermute | solution.py:394
